TPU v7x, 128 devices: a whole 4x4x4 slice. The times are simulated.
128 devices in a mesh: seq: 16 (over y, x), head: 2 (over core), dp: 4 (over z).
Axes of the slice: x: 4, y: 4, z: 4, core: 2. Of those that a mesh axis runs over, the one named last changes fastest.
Arguments:
- queries: bfloat16 [8192, 2048], P(('dp', 'seq', 'head')), parts along dimension 0, may hold values from -48 to 48
- keys: bfloat16 [8192, 2048], P(('dp', 'seq', 'head')), parts along dimension 0, may hold values from -4 to 4
- writes: bfloat16 [8192, 2048], P(('dp', 'seq', 'head')), parts along dimension 0, may hold values from -48 to 48
- values: bfloat16 [8192, 2048], P(('dp', 'seq', 'head')), parts along dimension 0, may hold values from -4 to 4
- starts: int32 [8192], P(('dp', 'seq')), parts along dimension 0, may hold values from 0 to 2047, as said below
Outputs:
- attended: bfloat16 [8192, 2048], P(('dp', 'seq', 'head')), parts along dimension 0
There are 4 independent parts, one for each index of `dp`. A program takes and returns all parts, laid end to end along the dimension named above; each array names one. Nothing has to cross between parts.
Inputs may be any that keep to these rules, and one draw needn't show every extreme that they name: starts[i] is the first position of position i's document: it never falls, is at most i, and equals i where a document begins.
All inputs are finite; a program needn't handle non-finite values.
Results may differ from a plain program's by a relative error of at most 0.004.
Values may be sent and summed in bfloat16 or wider, within the bound.
A program may use at most 64 MiB of HBM per device.

v0:
```python
from functools import partial

import jax
import jax.numpy as jnp
from jax import lax
from jax.sharding import PartitionSpec as P

HD = 128


masked_score = -1e30


def from_root(array, axis, root):
    return lax.dynamic_index_in_dim(lax.all_gather(array, axis), root, 0, keepdims=False)


def head_major(source, head_count):
    return source.reshape(source.shape[0], head_count, HD)


def pair_scores(queries_in, keys_in):
    return jnp.einsum(
        "ihd,jhd->hij", queries_in, keys_in, preferred_element_type=jnp.float32
    ) * HD ** (-0.5)


def key_masks(row_positions, doc_first, key_positions):
    after_start = key_positions[None, :] >= doc_first[:, None]
    strict_mask = (key_positions[None, :] < row_positions[:, None]) & after_start
    causal_mask = (key_positions[None, :] <= row_positions[:, None]) & after_start
    return (strict_mask, causal_mask)


def weights(score_rows, allowed, peak):
    return jnp.exp(jnp.where(allowed[None], score_rows - peak[:, :, None], masked_score))


def shards(queries, keys, writes, values, starts):
    query_local, key_local, write_local, value_local = (
        lax.all_to_all(queries, "head", split_axis=1, concat_axis=0, tiled=True),
        lax.all_to_all(keys, "head", split_axis=1, concat_axis=0, tiled=True),
        lax.all_to_all(writes, "head", split_axis=1, concat_axis=0, tiled=True),
        lax.all_to_all(values, "head", split_axis=1, concat_axis=0, tiled=True),
    )
    row_count = query_local.shape[0]
    feature_count = query_local.shape[1]
    head_count = feature_count // HD
    shard_count = lax.axis_size("seq")
    position = lax.axis_index("seq")
    query_head = head_major(query_local, head_count)
    write_head = head_major(write_local, head_count)
    all_keys = lax.all_gather(key_local, "seq", axis=0, tiled=True)
    key_blocks = all_keys.reshape(shard_count, row_count, head_count, HD)
    offsets = lax.iota(jnp.int32, row_count)
    row_positions = position * row_count + offsets

    def stat_step(step_index, carried):
        peak_write, total_write, peak_query, total_query = carried
        key_block = lax.dynamic_index_in_dim(key_blocks, step_index, 0, keepdims=False)
        strict_mask, causal_mask = key_masks(
            row_positions, starts, step_index * row_count + offsets
        )
        score_write = pair_scores(write_head, key_block)
        score_query = pair_scores(query_head, key_block)
        next_write = jnp.maximum(
            peak_write, jnp.max(jnp.where(strict_mask[None], score_write, masked_score), axis=2)
        )
        next_query = jnp.maximum(
            peak_query, jnp.max(jnp.where(causal_mask[None], score_query, masked_score), axis=2)
        )
        total_write = total_write * jnp.exp(peak_write - next_write) + jnp.sum(
            weights(score_write, strict_mask, next_write), axis=2
        )
        total_query = total_query * jnp.exp(peak_query - next_query) + jnp.sum(
            weights(score_query, causal_mask, next_query), axis=2
        )
        return (next_write, total_write, next_query, total_query)

    start_stats = (
        jnp.zeros((head_count, row_count), jnp.float32),
        jnp.ones((head_count, row_count), jnp.float32),
        jnp.full((head_count, row_count), masked_score, jnp.float32),
        jnp.zeros((head_count, row_count), jnp.float32),
    )
    peak_write, total_write, peak_query, total_query = lax.fori_loop(
        0, position + 1, stat_step, start_stats
    )
    own_strict, own_causal = key_masks(row_positions, starts, row_positions)
    own_keys = head_major(key_local, head_count)
    diagonal = (
        weights(pair_scores(write_head, own_keys), own_strict, peak_write) / total_write[:, :, None]
    )
    identity = jnp.broadcast_to(jnp.eye(row_count, dtype=jnp.float32), diagonal.shape)
    solver = jax.vmap(partial(jax.scipy.linalg.solve_triangular, lower=True, unit_diagonal=True))
    inverse = solver(diagonal, identity)
    value_rows = jnp.transpose(head_major(value_local, head_count), (1, 0, 2)).astype(jnp.float32)

    def read_block(score_query, allowed, arrived_u):
        weights_low = weights(score_query, allowed, peak_query).astype(jnp.bfloat16)
        return jnp.einsum(
            "hij,jhd->hid", weights_low, arrived_u, preferred_element_type=jnp.float32
        )

    def chain_step(step_index, carried):
        numerator, readout, own_solved = carried

        def solve_own(previous):
            right_side = value_rows - numerator / total_write[:, :, None]
            solved = jnp.einsum(
                "hij,hjd->hid",
                inverse,
                right_side,
                precision=lax.Precision.HIGHEST,
                preferred_element_type=jnp.float32,
            ).astype(jnp.bfloat16)
            return jnp.transpose(solved, (1, 0, 2)).reshape(row_count, feature_count)

        own_solved = lax.cond(
            step_index == position, solve_own, lambda previous: previous, own_solved
        )
        arrived = from_root(own_solved, "seq", step_index)

        def absorb(state):
            numer_now, read_now = state
            arrived_u = head_major(arrived, head_count)
            key_block = lax.dynamic_index_in_dim(key_blocks, step_index, 0, keepdims=False)
            strict_mask, causal_mask = key_masks(
                row_positions, starts, step_index * row_count + offsets
            )
            write_weights = weights(
                pair_scores(write_head, key_block), strict_mask, peak_write
            ).astype(jnp.bfloat16)
            numer_now = numer_now + jnp.einsum(
                "hij,jhd->hid", write_weights, arrived_u, preferred_element_type=jnp.float32
            )
            read_now = read_now + read_block(
                pair_scores(query_head, key_block), causal_mask, arrived_u
            )
            return (numer_now, read_now)

        numerator, readout = lax.cond(
            step_index <= position, absorb, lambda state: state, (numerator, readout)
        )
        return (numerator, readout, own_solved)

    zero_block = jnp.zeros((head_count, row_count, HD), jnp.float32)
    start_chain = (zero_block, zero_block, jnp.zeros((row_count, feature_count), jnp.bfloat16))
    numerator, readout, own_solved = lax.fori_loop(0, shard_count, chain_step, start_chain)
    mixed_out = (readout / total_query[:, :, None]).astype(jnp.bfloat16)
    mixed_out = jnp.transpose(mixed_out, (1, 0, 2)).reshape(row_count, feature_count)
    return lax.all_to_all(mixed_out, "head", split_axis=0, concat_axis=1, tiled=True)


def solution(mesh):
    in_specs = (
        P(("dp", "seq", "head"), None),
        P(("dp", "seq", "head"), None),
        P(("dp", "seq", "head"), None),
        P(("dp", "seq", "head"), None),
        P(("dp", "seq")),
    )
    out_specs = P(("dp", "seq", "head"), None)
    return jax.shard_map(shards, mesh=mesh, in_specs=in_specs, out_specs=out_specs, check_vma=False)
```

profile of v0, /device:TPU:1, one launch (start us, length us, event | category | flops | bytes accessed | tf_op | source)
XLA Modules:
  0.0 1228.2 jit_solution(8268921286809273200)
XLA Ops:
  6.5 1.0 copy.97
  7.6 5.7 all_to_all.83
  13.3 1.7 copy.96
  15.0 3.9 all-to-all-start.1
  18.9 1.7 copy.95
  20.6 3.5 all-to-all-start.2
  24.1 0.7 copy.94
  24.9 0.4 all-to-all-done.2
  25.2 3.8 all-to-all-start.3
  29.2 1.0 all-to-all-done.3
  30.4 0.2 copy.65
  30.8 35.8 %all-gather.7.cloned.1.call-done = bf16[2048,1024]{1,0:T(8,128)(2,1)} async-done(((bf16[128,1024]{1,0:T(8,128)(2,1)}), bf16[2048,1024]{1,0:T(8,128)(2,1)}) %all-gather.7.cloned.1.call-update) | async-done | bytes 4194320 | tf_op jit(solution)/shard_map/all_gather | solution.py:53
  66.7 3.3 copy.81
  70.0 3.2 copy.58
  73.2 3.0 while.38
  73.3 1.3 select_reduce_fusion.4
  74.7 1.3 select_reduce_fusion.5
  76.2 0.4 fusion.59
  76.6 78.6 %custom-call.4 = f32[8,1,128,128]{2,3,1,0:T(8,128)S(1)} custom-call(f32[8,1,128,128]{3,2,1,0:T(8,128)S(1)} %fusion.59), custom_call_target="InvertDiagBlocksLowerTriangular" | custom-call | tf_op jit(solution)/shard_map/vmap(jit(_solve_triangular))/triangular_solve | solution.py:96
  155.2 1.0 fusion.60
  156.3 1059.7 %while.39 = (s32[]{:T(128)}, f32[8,128,128]{2,1,0:T(8,128)S(1)}, f32[8,128,128]{2,1,0:T(8,128)S(1)}, bf16[128,1024]{0,1:T(8,128)(2,1)S(1)}, s32[]{:T(128)}, /*in...) while((s32[]{:T(128)}, f32[8,128,128]{2,1,0:T(8,128)S(1)}, ...), condition=%wide.region_11.12_spmd.clone, body=%wide.region_6.11_spmd.clone.sunk | while | flops 337330432 | bytes 29442524 | solution.py:149
  156.4 1.4 conditional.6
  156.4 0.2 copy.52
  156.6 1.2 convolution_convert_fusion
  157.8 0.9 copy.99
  158.7 95.2 %all-gather.9.cloned.1.call-done = bf16[2048,1024]{1,0:T(8,128)(2,1)} async-done(((bf16[128,1024]{1,0:T(8,128)(2,1)}), bf16[2048,1024]{1,0:T(8,128)(2,1)}) %all-gather.9.cloned.1.call-update) | async-done | bytes 4194320 | tf_op jit(solution)/shard_map/while/body/eval_jaxpr/all_gather | solution.py:15
  254.0 10.4 conditional.7
  254.0 6.3 copy.54
  260.3 1.0 constant_dynamic-slice_fusion
  261.4 1.5 convolution_add_fusion
  262.9 1.5 convolution_add_fusion.1
  264.5 0.9 copy.99
  265.3 53.0 %all-gather.9.cloned.1.call-done = bf16[2048,1024]{1,0:T(8,128)(2,1)} async-done(((bf16[128,1024]{1,0:T(8,128)(2,1)}), bf16[2048,1024]{1,0:T(8,128)(2,1)}) %all-gather.9.cloned.1.call-update) | async-done | bytes 4194320 | tf_op jit(solution)/shard_map/while/body/eval_jaxpr/all_gather | solution.py:15
  318.4 0.8 copy.99
  319.3 63.2 %all-gather.9.cloned.1.call-done = bf16[2048,1024]{1,0:T(8,128)(2,1)} async-done(((bf16[128,1024]{1,0:T(8,128)(2,1)}), bf16[2048,1024]{1,0:T(8,128)(2,1)}) %all-gather.9.cloned.1.call-update) | async-done | bytes 4194320 | tf_op jit(solution)/shard_map/while/body/eval_jaxpr/all_gather | solution.py:15
  382.5 0.8 copy.99
  383.3 63.2 %all-gather.9.cloned.1.call-done = bf16[2048,1024]{1,0:T(8,128)(2,1)} async-done(((bf16[128,1024]{1,0:T(8,128)(2,1)}), bf16[2048,1024]{1,0:T(8,128)(2,1)}) %all-gather.9.cloned.1.call-update) | async-done | bytes 4194320 | tf_op jit(solution)/shard_map/while/body/eval_jaxpr/all_gather | solution.py:15
  446.6 0.8 copy.99
  447.4 63.2 %all-gather.9.cloned.1.call-done = bf16[2048,1024]{1,0:T(8,128)(2,1)} async-done(((bf16[128,1024]{1,0:T(8,128)(2,1)}), bf16[2048,1024]{1,0:T(8,128)(2,1)}) %all-gather.9.cloned.1.call-update) | async-done | bytes 4194320 | tf_op jit(solution)/shard_map/while/body/eval_jaxpr/all_gather | solution.py:15
  510.7 0.8 copy.99
  511.5 63.5 %all-gather.9.cloned.1.call-done = bf16[2048,1024]{1,0:T(8,128)(2,1)} async-done(((bf16[128,1024]{1,0:T(8,128)(2,1)}), bf16[2048,1024]{1,0:T(8,128)(2,1)}) %all-gather.9.cloned.1.call-update) | async-done | bytes 4194320 | tf_op jit(solution)/shard_map/while/body/eval_jaxpr/all_gather | solution.py:15
  575.1 0.8 copy.99
  575.9 63.5 %all-gather.9.cloned.1.call-done = bf16[2048,1024]{1,0:T(8,128)(2,1)} async-done(((bf16[128,1024]{1,0:T(8,128)(2,1)}), bf16[2048,1024]{1,0:T(8,128)(2,1)}) %all-gather.9.cloned.1.call-update) | async-done | bytes 4194320 | tf_op jit(solution)/shard_map/while/body/eval_jaxpr/all_gather | solution.py:15
  639.5 0.8 copy.99
  640.3 63.5 %all-gather.9.cloned.1.call-done = bf16[2048,1024]{1,0:T(8,128)(2,1)} async-done(((bf16[128,1024]{1,0:T(8,128)(2,1)}), bf16[2048,1024]{1,0:T(8,128)(2,1)}) %all-gather.9.cloned.1.call-update) | async-done | bytes 4194320 | tf_op jit(solution)/shard_map/while/body/eval_jaxpr/all_gather | solution.py:15
  703.9 0.8 copy.99
  704.7 63.2 %all-gather.9.cloned.1.call-done = bf16[2048,1024]{1,0:T(8,128)(2,1)} async-done(((bf16[128,1024]{1,0:T(8,128)(2,1)}), bf16[2048,1024]{1,0:T(8,128)(2,1)}) %all-gather.9.cloned.1.call-update) | async-done | bytes 4194320 | tf_op jit(solution)/shard_map/while/body/eval_jaxpr/all_gather | solution.py:15
  768.0 0.8 copy.99
  768.8 63.5 %all-gather.9.cloned.1.call-done = bf16[2048,1024]{1,0:T(8,128)(2,1)} async-done(((bf16[128,1024]{1,0:T(8,128)(2,1)}), bf16[2048,1024]{1,0:T(8,128)(2,1)}) %all-gather.9.cloned.1.call-update) | async-done | bytes 4194320 | tf_op jit(solution)/shard_map/while/body/eval_jaxpr/all_gather | solution.py:15
  832.4 0.8 copy.99
  833.2 63.2 %all-gather.9.cloned.1.call-done = bf16[2048,1024]{1,0:T(8,128)(2,1)} async-done(((bf16[128,1024]{1,0:T(8,128)(2,1)}), bf16[2048,1024]{1,0:T(8,128)(2,1)}) %all-gather.9.cloned.1.call-update) | async-done | bytes 4194320 | tf_op jit(solution)/shard_map/while/body/eval_jaxpr/all_gather | solution.py:15
  896.4 0.8 copy.99
  897.3 63.5 %all-gather.9.cloned.1.call-done = bf16[2048,1024]{1,0:T(8,128)(2,1)} async-done(((bf16[128,1024]{1,0:T(8,128)(2,1)}), bf16[2048,1024]{1,0:T(8,128)(2,1)}) %all-gather.9.cloned.1.call-update) | async-done | bytes 4194320 | tf_op jit(solution)/shard_map/while/body/eval_jaxpr/all_gather | solution.py:15
  960.9 0.8 copy.99
  961.7 62.9 %all-gather.9.cloned.1.call-done = bf16[2048,1024]{1,0:T(8,128)(2,1)} async-done(((bf16[128,1024]{1,0:T(8,128)(2,1)}), bf16[2048,1024]{1,0:T(8,128)(2,1)}) %all-gather.9.cloned.1.call-update) | async-done | bytes 4194320 | tf_op jit(solution)/shard_map/while/body/eval_jaxpr/all_gather | solution.py:15
  1024.7 0.8 copy.99
  1025.5 62.9 %all-gather.9.cloned.1.call-done = bf16[2048,1024]{1,0:T(8,128)(2,1)} async-done(((bf16[128,1024]{1,0:T(8,128)(2,1)}), bf16[2048,1024]{1,0:T(8,128)(2,1)}) %all-gather.9.cloned.1.call-update) | async-done | bytes 4194320 | tf_op jit(solution)/shard_map/while/body/eval_jaxpr/all_gather | solution.py:15
  1088.5 0.8 copy.99
  1089.3 62.9 %all-gather.9.cloned.1.call-done = bf16[2048,1024]{1,0:T(8,128)(2,1)} async-done(((bf16[128,1024]{1,0:T(8,128)(2,1)}), bf16[2048,1024]{1,0:T(8,128)(2,1)}) %all-gather.9.cloned.1.call-update) | async-done | bytes 4194320 | tf_op jit(solution)/shard_map/while/body/eval_jaxpr/all_gather | solution.py:15
  1152.3 0.8 copy.99
  1153.1 62.9 %all-gather.9.cloned.1.call-done = bf16[2048,1024]{1,0:T(8,128)(2,1)} async-done(((bf16[128,1024]{1,0:T(8,128)(2,1)}), bf16[2048,1024]{1,0:T(8,128)(2,1)}) %all-gather.9.cloned.1.call-update) | async-done | bytes 4194320 | tf_op jit(solution)/shard_map/while/body/eval_jaxpr/all_gather | solution.py:15
  1216.1 0.2 fusion.64
  1216.6 4.4 all_to_all.84
  1221.0 0.7 copy.80
  (120 shorter events, 1.8 us)
Async XLA Ops:
  6.5 17.6 %copy-start.1 = (bf16[64,2048]{1,0:T(8,128)(2,1)S(1)}, bf16[64,2048]{1,0:T(8,128)(2,1)}, u32[]{:S(2)}) copy-start(bf16[64,2048]{1,0:T(8,128)(2,1)} %param.16) | copy-start | bytes 786436
  6.5 60.1 %all-gather.7.cloned.1.call-start = ((), (), s32[]{:S(2)}) async-start(), calls=%async_computation.5 | async-start | bytes 4456448 | tf_op jit(solution)/shard_map/all_gather | solution.py:53
  13.2 15.9 %copy-start = (bf16[64,2,1024]{2,0,1:T(8,128)(2,1)S(1)}, bf16[64,2,1024]{2,0,1:T(8,128)(2,1)}, u32[]{:S(2)}) copy-start(bf16[64,2,1024]{2,0,1:T(8,128)(2,1)} %all_to_all.83) | copy-start | bytes 786436
  15.0 15.7 %copy-start.2 = (s32[128]{0:T(128)S(1)}, s32[128]{0:T(128)}, u32[]{:S(2)}) copy-start(s32[128]{0:T(128)} %param.17) | copy-start | bytes 1540
  15.0 5.6 all-to-all-start.1
  20.6 4.7 all-to-all-start.2
  25.2 5.0 all-to-all-start.3
  156.3 97.6 %all-gather.9.cloned.1.call-start = ((), (), s32[]{:S(2)}) async-start(), calls=%async_computation.6 | async-start | bytes 4456448 | tf_op jit(solution)/shard_map/while/body/eval_jaxpr/all_gather | solution.py:15
  264.4 54.0 %all-gather.9.cloned.1.call-start = ((), (), s32[]{:S(2)}) async-start(), calls=%async_computation.6 | async-start | bytes 4456448 | tf_op jit(solution)/shard_map/while/body/eval_jaxpr/all_gather | solution.py:15
  318.4 64.1 %all-gather.9.cloned.1.call-start = ((), (), s32[]{:S(2)}) async-start(), calls=%async_computation.6 | async-start | bytes 4456448 | tf_op jit(solution)/shard_map/while/body/eval_jaxpr/all_gather | solution.py:15
  382.5 64.1 %all-gather.9.cloned.1.call-start = ((), (), s32[]{:S(2)}) async-start(), calls=%async_computation.6 | async-start | bytes 4456448 | tf_op jit(solution)/shard_map/while/body/eval_jaxpr/all_gather | solution.py:15
  446.6 64.1 %all-gather.9.cloned.1.call-start = ((), (), s32[]{:S(2)}) async-start(), calls=%async_computation.6 | async-start | bytes 4456448 | tf_op jit(solution)/shard_map/while/body/eval_jaxpr/all_gather | solution.py:15
  510.6 64.4 %all-gather.9.cloned.1.call-start = ((), (), s32[]{:S(2)}) async-start(), calls=%async_computation.6 | async-start | bytes 4456448 | tf_op jit(solution)/shard_map/while/body/eval_jaxpr/all_gather | solution.py:15
  575.1 64.4 %all-gather.9.cloned.1.call-start = ((), (), s32[]{:S(2)}) async-start(), calls=%async_computation.6 | async-start | bytes 4456448 | tf_op jit(solution)/shard_map/while/body/eval_jaxpr/all_gather | solution.py:15
  639.5 64.4 %all-gather.9.cloned.1.call-start = ((), (), s32[]{:S(2)}) async-start(), calls=%async_computation.6 | async-start | bytes 4456448 | tf_op jit(solution)/shard_map/while/body/eval_jaxpr/all_gather | solution.py:15
  703.9 64.1 %all-gather.9.cloned.1.call-start = ((), (), s32[]{:S(2)}) async-start(), calls=%async_computation.6 | async-start | bytes 4456448 | tf_op jit(solution)/shard_map/while/body/eval_jaxpr/all_gather | solution.py:15
  768.0 64.4 %all-gather.9.cloned.1.call-start = ((), (), s32[]{:S(2)}) async-start(), calls=%async_computation.6 | async-start | bytes 4456448 | tf_op jit(solution)/shard_map/while/body/eval_jaxpr/all_gather | solution.py:15
  832.4 64.1 %all-gather.9.cloned.1.call-start = ((), (), s32[]{:S(2)}) async-start(), calls=%async_computation.6 | async-start | bytes 4456448 | tf_op jit(solution)/shard_map/while/body/eval_jaxpr/all_gather | solution.py:15
  896.4 64.4 %all-gather.9.cloned.1.call-start = ((), (), s32[]{:S(2)}) async-start(), calls=%async_computation.6 | async-start | bytes 4456448 | tf_op jit(solution)/shard_map/while/body/eval_jaxpr/all_gather | solution.py:15
  960.9 63.8 %all-gather.9.cloned.1.call-start = ((), (), s32[]{:S(2)}) async-start(), calls=%async_computation.6 | async-start | bytes 4456448 | tf_op jit(solution)/shard_map/while/body/eval_jaxpr/all_gather | solution.py:15
  1024.7 63.8 %all-gather.9.cloned.1.call-start = ((), (), s32[]{:S(2)}) async-start(), calls=%async_computation.6 | async-start | bytes 4456448 | tf_op jit(solution)/shard_map/while/body/eval_jaxpr/all_gather | solution.py:15
  1088.5 63.8 %all-gather.9.cloned.1.call-start = ((), (), s32[]{:S(2)}) async-start(), calls=%async_computation.6 | async-start | bytes 4456448 | tf_op jit(solution)/shard_map/while/body/eval_jaxpr/all_gather | solution.py:15
  1152.3 63.8 %all-gather.9.cloned.1.call-start = ((), (), s32[]{:S(2)}) async-start(), calls=%async_computation.6 | async-start | bytes 4456448 | tf_op jit(solution)/shard_map/while/body/eval_jaxpr/all_gather | solution.py:15
Sparse Core Ops, SparseCore 0:
  13.4 53.2 all-gather.6
  159.3 94.6 all-gather.8
  267.3 50.9 all-gather.8
  321.0 61.4 all-gather.8
  385.1 61.4 all-gather.8
  449.2 61.4 all-gather.8
  513.6 61.4 all-gather.8
  578.0 61.4 all-gather.8
  642.4 61.4 all-gather.8
  706.5 61.4 all-gather.8
  770.9 61.4 all-gather.8
  835.0 61.4 all-gather.8
  899.4 61.4 all-gather.8
  963.5 61.1 all-gather.8
  1027.3 61.1 all-gather.8
  1091.1 61.1 all-gather.8
  1154.9 61.1 all-gather.8
where the time goes:
time: 1240 us; the launch traced here: 1230 us
  waiting for transfers between devices  1070 us (86%)
  other arithmetic  79.5 us (6%)
  local copies, waits for them, and re-layouts  34.4 us (3%)
  between operations  13.3 us (1%)
    all_gather x16, waiting for transfers between devices, from_root(): lax.all_gather(array, axis)  1030 us
    another operation x3, other arithmetic, shards(): inverse = solver(diagonal, identity)  78.7 us
    all_gather x1, waiting for transfers between devices, shards(): all_keys = lax.all_gather(key_local, 'seq', axis=0, tiled=True)  35.8 us
  transfers between devices with their start and end apart: 20, of which 19 were waited for; matrix products, arithmetic and copies ran while one was open for 0% of the time, Pallas kernels for 0%

commit v1 on v0

v1 whole, which is shorter than its diff:
```python
import functools
import math

import jax
import jax.numpy as jnp
from jax import lax
from jax.experimental import pallas as pl
from jax.experimental.pallas import tpu as pltpu
from jax.sharding import PartitionSpec as P

HD = 128
BLK = 128
HALF = 64
MASKED = -1e30
SCALE2 = HD ** (-0.5) * math.log2(math.e)
MESH = pl.DeviceIdType.MESH
F32 = jnp.float32
BF16 = jnp.bfloat16
NT = (((1,), (1,)), ((), ()))


def dot(a, b):
    return jnp.dot(a, b, preferred_element_type=F32)


def kernel(n, group, q_ref, k_ref, w_ref, v_ref, st_ref, out_ref, abuf, kbuf, vbuf, sbuf, ebuf, sscr,
           lbuf, xbuf, ubuf, uland, obuf, dbuf, send_sem, own_sem, st_send, recv_sem, st_recv, ku_send, u_recv,
           o_send, o_recv):
    me = lax.axis_index("seq")
    core = lax.axis_index("head")
    length = n * BLK

    def chip(step):
        return lax.rem(me + step, n)

    barrier = pltpu.get_barrier_semaphore()

    def greet(step, carry):
        for c in (0, 1):
            pl.semaphore_signal(barrier, inc=1, device_id={"seq": chip(step), "head": c}, device_id_type=MESH)
        return carry

    lax.fori_loop(1, n, greet, 0)
    pl.semaphore_signal(barrier, inc=1, device_id={"head": 1 - core}, device_id_type=MESH)
    pl.semaphore_wait(barrier, 2 * n - 1)

    my_rows = pl.ds(pl.multiple_of(me * BLK + core * HALF, HALF), HALF)
    streams = ((k_ref, kbuf, 0), (w_ref, abuf, 0), (v_ref, vbuf, 0), (q_ref, abuf, 1))

    def strip(ref, head):
        return ref.at[:, pl.ds(pl.multiple_of(head * HD, HD), HD)]

    def remote(stream, step):
        src, dst, c = streams[stream]
        target = chip(step)
        return pltpu.make_async_remote_copy(
            src_ref=strip(src, target), dst_ref=dst.at[my_rows], send_sem=send_sem.at[stream, step],
            recv_sem=recv_sem.at[stream], device_id={"seq": target, "head": c}, device_id_type=MESH)

    def starts_copy(step, c):
        return pltpu.make_async_remote_copy(
            src_ref=st_ref, dst_ref=sbuf.at[me], send_sem=st_send.at[step, c], recv_sem=st_recv,
            device_id={"seq": chip(step), "head": c}, device_id_type=MESH)

    for stream in range(4):
        src, dst, c = streams[stream]

        @pl.when(core == c)
        def _():
            pltpu.make_async_copy(strip(src, me), dst.at[my_rows], recv_sem.at[stream]).start()

        @pl.when(core != c)
        def _():
            remote(stream, 0).start()

        def send(step, carry):
            remote(stream, step).start()
            return carry

        lax.fori_loop(1, n, send, 0)
        if stream == 0:
            pltpu.make_async_copy(st_ref, sbuf.at[me], st_recv).start()
            for c in (0, 1):
                @pl.when(core == c)
                def _():
                    def send_starts(step, carry):
                        starts_copy(step, c).start()
                        return carry

                    lax.fori_loop(1, n, send_starts, 0)

    def wait_all(buf, sem):
        pltpu.make_async_copy(buf, buf, sem).wait()

    def keys_over():
        return pltpu.make_async_remote_copy(
            src_ref=kbuf, dst_ref=kbuf, send_sem=ku_send.at[n], recv_sem=recv_sem.at[4],
            device_id={"head": 1}, device_id_type=MESH)

    def solved_over(b):
        return pltpu.make_async_remote_copy(
            src_ref=ubuf.at[pl.ds(pl.multiple_of(b * BLK, BLK), BLK)], dst_ref=uland.at[b], send_sem=ku_send.at[b],
            recv_sem=u_recv.at[b], device_id={"head": 1}, device_id_type=MESH)

    def block_rows(b):
        return pl.ds(pl.multiple_of(b * BLK, BLK), BLK)

    def weights(solve):
        for g in range(n // group):
            def one(i, carry):
                b = g * group + i
                rows = abuf[block_rows(b), :]
                first = jnp.broadcast_to(sbuf[b].astype(F32), (BLK, BLK)).T.astype(jnp.int32)
                lane = lax.broadcasted_iota(jnp.int32, (BLK, BLK), 1)
                row = lax.broadcasted_iota(jnp.int32, (BLK, BLK), 0) + b * BLK
                top = jnp.full((BLK, BLK), 0.0 if solve else MASKED, F32)
                for j in range((g + 1) * group):
                    score = lax.dot_general(rows, kbuf[j * BLK:(j + 1) * BLK, :], NT, preferred_element_type=F32)
                    col = lane + j * BLK
                    allowed = col >= first
                    if j >= g * group:
                        allowed = allowed & ((col < row) if solve else (col <= row))
                    score = jnp.where(allowed, score, MASKED)
                    top = jnp.maximum(top, score)
                    sscr[:, j * BLK:(j + 1) * BLK] = score
                peak = jnp.max(top, axis=1, keepdims=True)
                total = jnp.zeros((BLK, BLK), F32)
                for j in range((g + 1) * group):
                    e = jnp.exp2((sscr[:, j * BLK:(j + 1) * BLK] - peak) * SCALE2)
                    total = total + e
                    ebuf[b, :, j * BLK:(j + 1) * BLK] = e.astype(BF16)
                    if solve and j >= g * group:
                        sscr[:, j * BLK:(j + 1) * BLK] = e
                den = jnp.sum(total, axis=1, keepdims=True)
                if solve:
                    den = den + jnp.exp2(-peak * SCALE2)
                inv = 1.0 / den
                dbuf[b] = jnp.broadcast_to(inv, (BLK, BLK))
                if solve:
                    lbuf[b] = sscr[:, block_rows(b)] * inv
                return carry

            lax.fori_loop(0, group, one, 0)

    def invert(b):
        low = lbuf[b]
        eye = (lax.broadcasted_iota(jnp.int32, (BLK, BLK), 0)
               == lax.broadcasted_iota(jnp.int32, (BLK, BLK), 1)).astype(F32)
        low_hi = low.astype(BF16)
        low_lo = (low - low_hi.astype(F32)).astype(BF16)
        total = eye - low
        power = dot(low_hi, low_hi).astype(BF16)
        for step in range(1, 7):
            if step < 6:
                both = dot(jnp.concatenate([total.astype(BF16), power], axis=0), power)
                total = total + both[:BLK]
                power = both[BLK:].astype(BF16)
            else:
                total = total + dot(total.astype(BF16), power)
        guess = total.astype(BF16)
        guess_wide = guess.astype(F32)
        residual = eye - guess_wide - dot(jnp.concatenate([low_hi, low_lo], axis=1),
                                          jnp.concatenate([guess, guess], axis=0))
        better = guess_wide + dot(guess, residual.astype(BF16))
        hi = better.astype(BF16)
        lo = (better - hi.astype(F32)).astype(BF16)
        xbuf[b] = jnp.concatenate([hi, lo, hi], axis=1)

    @pl.when(core == 0)
    def _():
        ubuf[...] = jnp.zeros_like(ubuf)
        wait_all(kbuf, recv_sem.at[0])
        keys_over().start()
        wait_all(sbuf, st_recv)
        wait_all(abuf, recv_sem.at[1])
        weights(True)

        def invert_some(i, carry):
            for j in range(4):
                invert(i * 4 + j)
            return carry

        lax.fori_loop(0, n // 4, invert_some, 0)
        wait_all(vbuf, recv_sem.at[2])
        for g in range(n // group):
            def one(i, carry):
                b = g * group + i
                width = (g + 1) * group * BLK
                numerator = dot(ebuf[b, :, 0:width], ubuf[0:width, :])
                rhs = vbuf[block_rows(b), :].astype(F32) - numerator * dbuf[b]
                hi = rhs.astype(BF16)
                lo = (rhs - hi.astype(F32)).astype(BF16)
                ubuf[block_rows(b), :] = dot(xbuf[b], jnp.concatenate([hi, hi, lo], axis=0)).astype(BF16)
                solved_over(b).start()
                return carry

            lax.fori_loop(0, group, one, 0)

    def readout_copy(b, half):
        return pltpu.make_async_remote_copy(
            src_ref=obuf.at[b, pl.ds(half * HALF, HALF)], dst_ref=strip(out_ref, me), send_sem=o_send.at[b, half],
            recv_sem=o_recv, device_id={"seq": b, "head": half}, device_id_type=MESH)

    @pl.when(core == 1)
    def _():
        ubuf[...] = jnp.zeros_like(ubuf)
        wait_all(sbuf, st_recv)
        wait_all(abuf, recv_sem.at[3])
        wait_all(kbuf, recv_sem.at[4])
        weights(False)
        for g in range(n // group):
            def one(i, carry):
                b = g * group + i
                width = (g + 1) * group * BLK
                wait_all(uland.at[b], u_recv.at[b])
                ubuf[block_rows(b), :] = uland[b]
                numerator = dot(ebuf[b, :, 0:width], ubuf[0:width, :])
                obuf[b] = (numerator * dbuf[b]).astype(BF16)
                readout_copy(b, 0).start()

                @pl.when(b != me)
                def _():
                    readout_copy(b, 1).start()

                @pl.when(b == me)
                def _():
                    pltpu.make_async_copy(obuf.at[b, pl.ds(HALF, HALF)], strip(out_ref, me), o_recv).start()

                return carry

            lax.fori_loop(0, group, one, 0)

    wait_all(out_ref, o_recv)

    for stream in range(4):
        @pl.when(core != streams[stream][2])
        def _():
            remote(stream, 0).wait_send()

        def sent(step, carry):
            remote(stream, step).wait_send()
            return carry

        lax.fori_loop(1, n, sent, 0)
    for c in (0, 1):
        @pl.when(core == c)
        def _():
            def starts_sent(step, carry):
                starts_copy(step, c).wait_send()
                return carry

            lax.fori_loop(1, n, starts_sent, 0)

    @pl.when(core == 0)
    def _():
        keys_over().wait_send()

        def solved_sent(b, carry):
            solved_over(b).wait_send()
            return carry

        lax.fori_loop(0, n, solved_sent, 0)

    @pl.when(core == 1)
    def _():
        def readout_sent(b, carry):
            readout_copy(b, 0).wait_send()

            @pl.when(b != me)
            def _():
                readout_copy(b, 1).wait_send()

            return carry

        lax.fori_loop(0, n, readout_sent, 0)


def solution(mesh):
    n = mesh.shape["seq"]
    group = 4

    def step(queries, keys, writes, values, starts):
        features = queries.shape[1]
        length = n * BLK
        hbm = pl.BlockSpec(memory_space=pl.ANY)
        dma = pltpu.SemaphoreType.DMA
        return pl.pallas_call(
            functools.partial(kernel, n, group),
            out_shape=jax.ShapeDtypeStruct((HALF, features), BF16),
            in_specs=[hbm] * 5,
            out_specs=hbm,
            scratch_shapes=[
                pltpu.VMEM((length, HD), BF16),
                pltpu.VMEM((length, HD), BF16),
                pltpu.VMEM((length, HD), BF16),
                pltpu.VMEM((n, 1, BLK), jnp.int32),
                pltpu.VMEM((n, BLK, length), BF16),
                pltpu.VMEM((BLK, length), F32),
                pltpu.VMEM((n, BLK, BLK), F32),
                pltpu.VMEM((n, BLK, 3 * BLK), BF16),
                pltpu.VMEM((length, HD), BF16),
                pltpu.VMEM((n, BLK, HD), BF16),
                pltpu.VMEM((n, BLK, HD), BF16),
                pltpu.VMEM((n, BLK, BLK), F32),
                dma((4, n)),
                dma,
                dma((n, 2)),
                dma((5,)),
                dma,
                dma((n + 1,)),
                dma((n,)),
                dma((n, 2)),
                dma,
            ],
            compiler_params=pltpu.CompilerParams(collective_id=0, has_side_effects=True,
                                                 vmem_limit_bytes=48 * 1024 * 1024),
        )(queries, keys, writes, values, starts.reshape(1, BLK))

    rows = P(("dp", "seq", "head"), None)
    return jax.shard_map(step, mesh=mesh, in_specs=(rows, rows, rows, rows, P(("dp", "seq"))), out_specs=rows,
                         check_vma=False)
```

time: 1240 us -> 62.3 us (0.05)
  waiting for transfers between devices: 1070 us -> 0 us
  other arithmetic: 79.5 us -> 0 us
  Pallas kernels: 0 us -> 56.7 us
  local copies, waits for them, and re-layouts: 34.4 us -> 5.16 us
  between operations: 13.3 us -> 0.01 us
    all_gather x17 -> x0, waiting for transfers between devices: 1070 us -> none  [the longest x16 1030 us: from_root(): lax.all_gather(array, axis)]
    another operation x3 -> x0, other arithmetic: 78.7 us -> none  [shards(): inverse = solver(diagonal, identity)]
    pallas_call x0 -> x1, Pallas kernels: none -> 56.7 us  [step(): pl.pallas_call(functools.partial(kernel, n, group), out_shape=jax.ShapeDt...]
    cond x16 -> x0, local copies, waits for them, and re-layouts: 13.6 us -> none  [chain_step(): lax.cond(step_index == position, solve_own, lambda previous: previous, ow...]
  transfers between devices with their start and end apart: 20 -> 0, of which waited for: 19 -> 0; matrix products, arithmetic and copies ran while one was open for 0% -> 0% of each run, Pallas kernels for 0% -> 0%
where the time goes in v1:
time: 62.3 us; the launch traced here: 61.9 us
  Pallas kernels  56.7 us (91%)
  local copies, waits for them, and re-layouts  5.16 us (8%)
    pallas_call x1, Pallas kernels, step(): pl.pallas_call(functools.partial(kernel, n, group), out_shape=jax.ShapeDt...  56.7 us
    unnamed x11, local copies, waits for them, and re-layouts  5.16 us

profile of v1, /device:TPU:1, one launch (start us, length us, event | category | flops | bytes accessed | tf_op | source)
XLA Modules:
  0.0 61.9 jit_solution(3790850469467425138)
XLA Ops:
  0.0 0.0 copy-start.4
  0.0 0.7 %copy-done.4 = s32[128]{0:T(128)S(1)} copy-done((s32[128]{0:T(128)S(1)}, s32[128]{0:T(128)}, u32[]{:S(2)}) %copy-start.4) | copy-done | bytes 536
  0.7 0.0 copy-start
  0.7 0.9 %copy-done = bf16[64,2048]{1,0:T(8,128)(2,1)S(1)} copy-done((bf16[64,2048]{1,0:T(8,128)(2,1)S(1)}, bf16[64,2048]{1,0:T(8,128)(2,1)}, u32[]{:S(2)}) %copy-start) | copy-done | bytes 262168
  1.6 0.0 copy-start.1
  1.6 0.9 %copy-done.1 = bf16[64,2048]{1,0:T(8,128)(2,1)S(1)} copy-done((bf16[64,2048]{1,0:T(8,128)(2,1)S(1)}, bf16[64,2048]{1,0:T(8,128)(2,1)}, u32[]{:S(2)}) %copy-start.1) | copy-done | bytes 262168
  2.6 0.0 copy-start.2
  2.6 0.9 %copy-done.2 = bf16[64,2048]{1,0:T(8,128)(2,1)S(1)} copy-done((bf16[64,2048]{1,0:T(8,128)(2,1)S(1)}, bf16[64,2048]{1,0:T(8,128)(2,1)}, u32[]{:S(2)}) %copy-start.2) | copy-done | bytes 262168
  3.5 0.0 copy-start.3
  3.5 0.9 %copy-done.3 = bf16[64,2048]{1,0:T(8,128)(2,1)S(1)} copy-done((bf16[64,2048]{1,0:T(8,128)(2,1)S(1)}, bf16[64,2048]{1,0:T(8,128)(2,1)}, u32[]{:S(2)}) %copy-start.3) | copy-done | bytes 262168
  4.5 56.7 %shard_map.55 = bf16[64,2048]{1,0:T(8,128)(2,1)S(1)} custom-call(bf16[64,2048]{1,0:T(8,128)(2,1)S(1)} %copy-done, bf16[64,2048]{1,0:T(8,128)(2,1)S(1)} %copy-done.1, bf16[64,2048]{1,0:T(8,128)(2,1)S(1)} %copy-done.2, bf16[64,2048]{1,0:T(8,128)(2,1)S(1)} %copy-done.3, s32[1,128]{1,0:T(1,128)S(1)} %bitcast.1), custom_call_target="tpu_custom_call" | custom-call | tf_op jit(solution)/shard_map/pallas_call | solution.py:287
  61.2 0.7 %copy.7 = bf16[64,2048]{1,0:T(8,128)(2,1)} copy(bf16[64,2048]{1,0:T(8,128)(2,1)S(1)} %shard_map.55) | data formatting | bytes 524288
Async XLA Ops:
  0.0 0.7 %copy-start.4 = (s32[128]{0:T(128)S(1)}, s32[128]{0:T(128)}, u32[]{:S(2)}) copy-start(s32[128]{0:T(128)} %param.9) | copy-start | bytes 1540
  0.7 0.9 %copy-start = (bf16[64,2048]{1,0:T(8,128)(2,1)S(1)}, bf16[64,2048]{1,0:T(8,128)(2,1)}, u32[]{:S(2)}) copy-start(bf16[64,2048]{1,0:T(8,128)(2,1)} %q_ref.1) | copy-start | bytes 786436
  1.6 0.9 %copy-start.1 = (bf16[64,2048]{1,0:T(8,128)(2,1)S(1)}, bf16[64,2048]{1,0:T(8,128)(2,1)}, u32[]{:S(2)}) copy-start(bf16[64,2048]{1,0:T(8,128)(2,1)} %k_ref.1) | copy-start | bytes 786436
  2.6 0.9 %copy-start.2 = (bf16[64,2048]{1,0:T(8,128)(2,1)S(1)}, bf16[64,2048]{1,0:T(8,128)(2,1)}, u32[]{:S(2)}) copy-start(bf16[64,2048]{1,0:T(8,128)(2,1)} %w_ref.1) | copy-start | bytes 786436
  3.5 0.9 %copy-start.3 = (bf16[64,2048]{1,0:T(8,128)(2,1)S(1)}, bf16[64,2048]{1,0:T(8,128)(2,1)}, u32[]{:S(2)}) copy-start(bf16[64,2048]{1,0:T(8,128)(2,1)} %v_ref.1) | copy-start | bytes 786436

commit v2 on v1

v2 whole, which is shorter than its diff:
```python
import functools
import math

import jax
import jax.numpy as jnp
from jax import lax
from jax.experimental import pallas as pl
from jax.experimental.pallas import tpu as pltpu
from jax.sharding import PartitionSpec as P

HD = 128
BLK = 128
HALF = 64
MASKED = -1e30
SCALE2 = HD ** (-0.5) * math.log2(math.e)
MESH = pl.DeviceIdType.MESH
F32 = jnp.float32
BF16 = jnp.bfloat16
NT = (((1,), (1,)), ((), ()))


def dot(a, b):
    return jnp.dot(a, b, preferred_element_type=F32)


def kernel(n, q_ref, k_ref, w_ref, v_ref, st_ref, out_ref, abuf, kbuf, vbuf, sbuf, ebuf, sscr, mbuf, ybuf, ubuf,
           obuf, dbuf, send_sem, st_send, recv_sem, st_recv, ku_send, u_recv, o_send, o_recv):
    me = lax.axis_index("seq")
    core = lax.axis_index("head")

    def chip(step):
        return lax.rem(me + step, n)

    barrier = pltpu.get_barrier_semaphore()

    def greet(step, carry):
        for c in (0, 1):
            pl.semaphore_signal(barrier, inc=1, device_id={"seq": chip(step), "head": c}, device_id_type=MESH)
        return carry

    lax.fori_loop(1, n, greet, 0)
    pl.semaphore_signal(barrier, inc=1, device_id={"head": 1 - core}, device_id_type=MESH)
    pl.semaphore_wait(barrier, 2 * n - 1)

    my_rows = pl.ds(pl.multiple_of(me * BLK + core * HALF, HALF), HALF)
    streams = ((k_ref, kbuf, 0), (w_ref, abuf, 0), (v_ref, vbuf, 0), (q_ref, abuf, 1))

    def strip(ref, head):
        return ref.at[:, pl.ds(pl.multiple_of(head * HD, HD), HD)]

    def remote(stream, step):
        src, dst, c = streams[stream]
        target = chip(step)
        return pltpu.make_async_remote_copy(
            src_ref=strip(src, target), dst_ref=dst.at[my_rows], send_sem=send_sem.at[stream, step],
            recv_sem=recv_sem.at[stream], device_id={"seq": target, "head": c}, device_id_type=MESH)

    def starts_copy(step, c):
        return pltpu.make_async_remote_copy(
            src_ref=st_ref, dst_ref=sbuf.at[me], send_sem=st_send.at[step, c], recv_sem=st_recv,
            device_id={"seq": chip(step), "head": c}, device_id_type=MESH)

    for stream in range(4):
        src, dst, c = streams[stream]

        @pl.when(core == c)
        def _():
            pltpu.make_async_copy(strip(src, me), dst.at[my_rows], recv_sem.at[stream]).start()

        @pl.when(core != c)
        def _():
            remote(stream, 0).start()

        def send(step, carry):
            remote(stream, step).start()
            return carry

        lax.fori_loop(1, n, send, 0)
        if stream == 0:
            pltpu.make_async_copy(st_ref, sbuf.at[me], st_recv).start()
            for c in (0, 1):
                @pl.when(core == c)
                def _():
                    def send_starts(step, carry):
                        starts_copy(step, c).start()
                        return carry

                    lax.fori_loop(1, n, send_starts, 0)

    def wait_all(buf, sem):
        pltpu.make_async_copy(buf, buf, sem).wait()

    def keys_over():
        return pltpu.make_async_remote_copy(
            src_ref=kbuf, dst_ref=kbuf, send_sem=ku_send.at[n], recv_sem=recv_sem.at[4],
            device_id={"head": 1}, device_id_type=MESH)

    def solved_over(p):
        return pltpu.make_async_remote_copy(
            src_ref=ubuf.at[p], dst_ref=ubuf.at[p], send_sem=ku_send.at[p], recv_sem=u_recv.at[p],
            device_id={"head": 1}, device_id_type=MESH)

    pairs = n // 2
    wide = 2 * BLK

    def weights(p, solve):
        rows = abuf[p * wide:(p + 1) * wide, :]
        sub = lax.broadcasted_iota(jnp.int32, (8, wide), 0)
        first = jnp.concatenate([sbuf[2 * p], sbuf[2 * p + 1]], axis=1) - sub
        limit = lax.broadcasted_iota(jnp.int32, (8, wide), 1) + p * wide - sub
        top = jnp.full((8, wide), 0.0 if solve else MASKED, F32)
        tiles = 2 * p + 2
        for j in range(tiles):
            score = lax.dot_general(kbuf[j * BLK:(j + 1) * BLK, :], rows, NT, preferred_element_type=F32)
            score = score.reshape(BLK // 8, 8, wide)
            key = lax.broadcasted_iota(jnp.int32, score.shape, 0) * 8 + j * BLK
            allowed = key >= first
            if j >= 2 * p:
                allowed = allowed & ((key < limit) if solve else (key <= limit))
            score = jnp.where(allowed, score, MASKED)
            top = jnp.maximum(top, jnp.max(score, axis=0))
            sscr[j * BLK:(j + 1) * BLK, :] = score.reshape(BLK, wide)
        peak = jnp.max(top, axis=0, keepdims=True)
        total = jnp.zeros((8, wide), F32)
        for j in range(tiles):
            e = jnp.exp2((sscr[j * BLK:(j + 1) * BLK, :] - peak) * SCALE2)
            total = total + jnp.sum(e.reshape(BLK // 8, 8, wide), axis=0)
            ebuf[p, j * BLK:(j + 1) * BLK, :] = e.astype(BF16)
            if solve and j >= 2 * p:
                mbuf[p, (j - 2 * p) * BLK:(j - 2 * p + 1) * BLK, :] = e
        den = jnp.sum(total, axis=0, keepdims=True)
        if solve:
            den = den + jnp.exp2(-peak * SCALE2)
        dbuf[p] = 1.0 / den
        if solve:
            mbuf[p] = mbuf[p] * dbuf[p]

    def diagonal(x):
        zero = jnp.zeros((BLK, BLK), BF16)
        return jnp.concatenate([jnp.concatenate([x[:, :BLK], zero], axis=1),
                                jnp.concatenate([zero, x[:, BLK:]], axis=1)], axis=0)

    def split(x):
        hi = x.astype(BF16)
        return hi, (x - hi.astype(F32)).astype(BF16)

    def product(a, b):
        (a_hi, a_lo), (b_hi, b_lo) = split(a), split(b)
        return dot(jnp.concatenate([a_hi, a_lo, a_hi], axis=1), jnp.concatenate([b_hi, b_hi, b_lo], axis=0))

    def invert(which):
        eye = (lax.broadcasted_iota(jnp.int32, (BLK, BLK), 0)
               == lax.broadcasted_iota(jnp.int32, (BLK, BLK), 1)).astype(F32)
        eye = jnp.concatenate([eye, eye], axis=1)
        upper = {p: jnp.concatenate([mbuf[p, :BLK, :BLK], mbuf[p, BLK:, BLK:]], axis=1) for p in which}
        parts = {p: split(upper[p]) for p in which}
        total = {p: eye - upper[p] for p in which}
        power = {p: dot(parts[p][0], diagonal(parts[p][0])).astype(BF16) for p in which}
        for step in range(1, 7):
            for p in which:
                if step < 6:
                    both = dot(jnp.concatenate([total[p].astype(BF16), power[p]], axis=0), diagonal(power[p]))
                    total[p] = total[p] + both[:BLK]
                    power[p] = both[BLK:].astype(BF16)
                else:
                    total[p] = total[p] + dot(total[p].astype(BF16), diagonal(power[p]))
        guess = {p: total[p].astype(BF16) for p in which}
        again = {p: dot(jnp.concatenate(parts[p], axis=0), diagonal(guess[p])) for p in which}
        better = {}
        for p in which:
            residual = eye - guess[p].astype(F32) - again[p][:BLK] - again[p][BLK:]
            better[p] = guess[p].astype(F32) + dot(guess[p], diagonal(residual.astype(BF16)))
        inner = {p: product(mbuf[p, :BLK, BLK:], better[p][:, BLK:]) for p in which}
        for p in which:
            corner = -product(better[p][:, :BLK], inner[p])
            whole = jnp.concatenate(
                [jnp.concatenate([better[p][:, :BLK], corner], axis=1),
                 jnp.concatenate([jnp.zeros((BLK, BLK), F32), better[p][:, BLK:]], axis=1)], axis=0)
            hi, lo = split(whole)
            ybuf[p, :wide] = hi
            ybuf[p, wide:2 * wide] = hi
            ybuf[p, 2 * wide:] = lo

    def solved(count):
        return jnp.concatenate([ubuf[q] for q in range(count)], axis=1)

    @pl.when(core == 0)
    def _():
        wait_all(kbuf, recv_sem.at[0])
        keys_over().start()
        wait_all(sbuf, st_recv)
        wait_all(abuf, recv_sem.at[1])
        for p in range(pairs):
            weights(p, True)
        for g in range(0, pairs, 4):
            invert(range(g, min(g + 4, pairs)))
        wait_all(vbuf, recv_sem.at[2])
        for p in range(pairs):
            rhs = vbuf[p * wide:(p + 1) * wide, :].astype(F32).T
            if p:
                rhs = rhs - dot(solved(p), ebuf[p, :p * wide, :]) * dbuf[p]
            hi, lo = split(rhs)
            ubuf[p] = dot(jnp.concatenate([hi, lo, hi], axis=1), ybuf[p]).astype(BF16)
            solved_over(p).start()

    def readout_copy(p, r, half):
        return pltpu.make_async_remote_copy(
            src_ref=obuf.at[p, pl.ds((2 * r + half) * HALF, HALF)], dst_ref=strip(out_ref, me),
            send_sem=o_send.at[2 * p + r, half], recv_sem=o_recv, device_id={"seq": 2 * p + r, "head": half},
            device_id_type=MESH)

    @pl.when(core == 1)
    def _():
        wait_all(sbuf, st_recv)
        wait_all(abuf, recv_sem.at[3])
        wait_all(kbuf, recv_sem.at[4])
        for p in range(pairs):
            weights(p, False)
        for p in range(pairs):
            if p:
                before = dot(solved(p), ebuf[p, :p * wide, :])
            wait_all(ubuf.at[p], u_recv.at[p])
            read = dot(ubuf[p], ebuf[p, p * wide:(p + 1) * wide, :])
            if p:
                read = read + before
            obuf[p] = (read * dbuf[p]).T.astype(BF16)
            for r in (0, 1):
                readout_copy(p, r, 0).start()

                @pl.when(me != 2 * p + r)
                def _():
                    readout_copy(p, r, 1).start()

                @pl.when(me == 2 * p + r)
                def _():
                    pltpu.make_async_copy(obuf.at[p, pl.ds((2 * r + 1) * HALF, HALF)], strip(out_ref, me),
                                          o_recv).start()

    wait_all(out_ref, o_recv)

    for stream in range(4):
        @pl.when(core != streams[stream][2])
        def _():
            remote(stream, 0).wait_send()

        def sent(step, carry):
            remote(stream, step).wait_send()
            return carry

        lax.fori_loop(1, n, sent, 0)
    for c in (0, 1):
        @pl.when(core == c)
        def _():
            def starts_sent(step, carry):
                starts_copy(step, c).wait_send()
                return carry

            lax.fori_loop(1, n, starts_sent, 0)

    @pl.when(core == 0)
    def _():
        keys_over().wait_send()

        def solved_sent(p, carry):
            solved_over(p).wait_send()
            return carry

        lax.fori_loop(0, pairs, solved_sent, 0)

    @pl.when(core == 1)
    def _():
        for p in range(pairs):
            for r in (0, 1):
                readout_copy(p, r, 0).wait_send()

                @pl.when(me != 2 * p + r)
                def _():
                    readout_copy(p, r, 1).wait_send()


def solution(mesh):
    n = mesh.shape["seq"]

    def step(queries, keys, writes, values, starts):
        features = queries.shape[1]
        length = n * BLK
        hbm = pl.BlockSpec(memory_space=pl.ANY)
        dma = pltpu.SemaphoreType.DMA
        return pl.pallas_call(
            functools.partial(kernel, n),
            out_shape=jax.ShapeDtypeStruct((HALF, features), BF16),
            in_specs=[hbm] * 5,
            out_specs=hbm,
            scratch_shapes=[
                pltpu.VMEM((length, HD), BF16),
                pltpu.VMEM((length, HD), BF16),
                pltpu.VMEM((length, HD), BF16),
                pltpu.VMEM((n, 1, BLK), jnp.int32),
                pltpu.VMEM((n // 2, length, 2 * BLK), BF16),
                pltpu.VMEM((length, 2 * BLK), F32),
                pltpu.VMEM((n // 2, 2 * BLK, 2 * BLK), F32),
                pltpu.VMEM((n // 2, 6 * BLK, 2 * BLK), BF16),
                pltpu.VMEM((n // 2, HD, 2 * BLK), BF16),
                pltpu.VMEM((n // 2, 2 * BLK, HD), BF16),
                pltpu.VMEM((n // 2, 1, 2 * BLK), F32),
                dma((4, n)),
                dma((n, 2)),
                dma((5,)),
                dma,
                dma((n + 1,)),
                dma((n // 2,)),
                dma((n, 2)),
                dma,
            ],
            compiler_params=pltpu.CompilerParams(collective_id=0, has_side_effects=True,
                                                 vmem_limit_bytes=67_043_328),
        )(queries, keys, writes, values, starts.reshape(1, BLK))

    rows = P(("dp", "seq", "head"), None)
    return jax.shard_map(step, mesh=mesh, in_specs=(rows, rows, rows, rows, P(("dp", "seq"))), out_specs=rows,
                         check_vma=False)
```

time: 62.3 us -> 34.7 us (0.56)
  Pallas kernels: 56.7 us -> 32.9 us
  local copies, waits for them, and re-layouts: 5.16 us -> 1.67 us
    pallas_call x1, Pallas kernels: 56.7 us -> 32.9 us  [step(): pl.pallas_call(functools.partial(kernel, n), out_shape=jax.ShapeDtypeStru...]
    unnamed x11 -> x1, local copies, waits for them, and re-layouts: 5.16 us -> 1.67 us
where the time goes in v2:
time: 34.7 us; the launch traced here: 34.6 us
  Pallas kernels  32.9 us (95%)
  local copies, waits for them, and re-layouts  1.67 us (5%)
    pallas_call x1, Pallas kernels, step(): pl.pallas_call(functools.partial(kernel, n), out_shape=jax.ShapeDtypeStru...  32.9 us
    unnamed x1, local copies, waits for them, and re-layouts  1.67 us

profile of v2, /device:TPU:1, one launch (start us, length us, event | category | flops | bytes accessed | tf_op | source)
XLA Modules:
  0.0 34.6 jit_solution(7587942777080841842)
XLA Ops:
  0.0 32.9 %shard_map.55 = bf16[64,2048]{1,0:T(8,128)(2,1)} custom-call(bf16[64,2048]{1,0:T(8,128)(2,1)} %q_ref.1, bf16[64,2048]{1,0:T(8,128)(2,1)} %k_ref.1, bf16[64,2048]{1,0:T(8,128)(2,1)} %w_ref.1, bf16[64,2048]{1,0:T(8,128)(2,1)} %v_ref.1, s32[1,128]{1,0:T(1,128)} %bitcast.1), custom_call_target="tpu_custom_call" | custom-call | tf_op jit(solution)/shard_map/pallas_call | solution.py:289
  32.9 1.7 %copy.7 = bf16[64,2048]{1,0:T(8,128)(2,1)} copy(bf16[64,2048]{1,0:T(8,128)(2,1)} %shard_map.55) | data formatting | bytes 524288

commit v3 on v2

v3 whole, which is shorter than its diff:
```python
import functools
import math

import jax
import jax.numpy as jnp
from jax import lax
from jax.experimental import pallas as pl
from jax.experimental.pallas import tpu as pltpu
from jax.sharding import PartitionSpec as P

HD = 128
BLK = 128
HALF = 64
MASKED = -1e30
SCALE2 = HD ** (-0.5) * math.log2(math.e)
MESH = pl.DeviceIdType.MESH
F32 = jnp.float32
BF16 = jnp.bfloat16
NT = (((1,), (1,)), ((), ()))


def dot(a, b):
    return jnp.dot(a, b, preferred_element_type=F32)


def kernel(n, q_ref, k_ref, w_ref, v_ref, st_ref, out_ref, qbuf, kbuf, wbuf, vbuf, sbuf, bias, ebuf, fbuf, sscr, mbuf,
           ybuf, ubuf, obuf, dbuf, fden, send_sem, st_send, recv_sem, k_send, k_recv, st_recv, u_send, u_recv, o_send,
           o_recv):
    me = lax.axis_index("seq")
    core = lax.axis_index("head")

    def chip(step):
        return lax.rem(me + step, n)

    barrier = pltpu.get_barrier_semaphore()

    def greet(step, carry):
        for c in (0, 1):
            pl.semaphore_signal(barrier, inc=1, device_id={"seq": chip(step), "head": c}, device_id_type=MESH)
        return carry

    lax.fori_loop(1, n, greet, 0)
    pl.semaphore_signal(barrier, inc=1, device_id={"head": 1 - core}, device_id_type=MESH)
    pl.semaphore_wait(barrier, 2 * n - 1)

    my_rows = pl.ds(pl.multiple_of(me * BLK + core * HALF, HALF), HALF)
    half_index = me // (n // 2)
    solver = 1 - half_index
    reader = jnp.where(me >= n - 2, 0, 1)
    streams = ((k_ref, kbuf, solver), (w_ref, wbuf, solver), (v_ref, vbuf, solver), (q_ref, qbuf, reader))

    def strip(ref, head):
        return ref.at[:, pl.ds(pl.multiple_of(head * HD, HD), HD)]

    def remote(stream, step):
        src, dst, c = streams[stream]
        target = chip(step)
        return pltpu.make_async_remote_copy(
            src_ref=strip(src, target), dst_ref=dst.at[my_rows], send_sem=send_sem.at[stream, step],
            recv_sem=recv_sem.at[stream, half_index], device_id={"seq": target, "head": c}, device_id_type=MESH)

    def starts_copy(step, c):
        return pltpu.make_async_remote_copy(
            src_ref=st_ref, dst_ref=sbuf.at[me], send_sem=st_send.at[step, c], recv_sem=st_recv,
            device_id={"seq": chip(step), "head": c}, device_id_type=MESH)

    pltpu.make_async_copy(st_ref, sbuf.at[me], st_recv).start()
    for c in (0, 1):
        @pl.when(core == c)
        def _():
            def send_starts(step, carry):
                starts_copy(step, c).start()
                return carry

            lax.fori_loop(1, n, send_starts, 0)

    def send_stream(stream):
        src, dst, c = streams[stream]

        @pl.when(core == c)
        def _():
            pltpu.make_async_copy(strip(src, me), dst.at[my_rows], recv_sem.at[stream, half_index]).start()

        @pl.when(core != c)
        def _():
            remote(stream, 0).start()

        def send(step, carry):
            remote(stream, step).start()
            return carry

        lax.fori_loop(1, n, send, 0)

    send_stream(0)
    send_stream(1)

    @pl.when(half_index == 0)
    def _():
        send_stream(2)
        send_stream(3)

    @pl.when(half_index != 0)
    def _():
        send_stream(3)
        send_stream(2)

    def wait_all(buf, sem):
        pltpu.make_async_copy(buf, buf, sem).wait()

    def wait_rows(buf, stream, first, last):
        if last > first:
            wait_all(buf.at[first * BLK:last * BLK], recv_sem.at[stream, first // (n // 2)])

    def keys_over():
        mine = kbuf.at[pl.ds(pl.multiple_of((1 - core) * (n * HALF), n * HALF), n * HALF)]
        return pltpu.make_async_remote_copy(src_ref=mine, dst_ref=mine, send_sem=k_send, recv_sem=k_recv,
                                            device_id={"head": 1 - core}, device_id_type=MESH)

    def solved_over(p):
        return pltpu.make_async_remote_copy(
            src_ref=ubuf.at[p], dst_ref=ubuf.at[p], send_sem=u_send.at[p], recv_sem=u_recv.at[p],
            device_id={"head": 1 - core}, device_id_type=MESH)

    pairs = n // 2
    wide = 2 * BLK

    half_pairs = pairs // 2

    def tile_of(p, j):
        return p * (p + 1) + j

    def mask(which):
        for p in which:
            first = jnp.concatenate([sbuf[2 * p], sbuf[2 * p + 1]], axis=1)
            first = first - lax.broadcasted_iota(jnp.int32, (8, wide), 0)
            for j in range(2 * p + 2):
                key = lax.broadcasted_iota(jnp.int32, (BLK // 8, 8, wide), 0) * 8 + j * BLK
                bias[tile_of(p, j)] = jnp.where(key >= first, 0.0, MASKED).reshape(BLK, wide)

    def weights(p, solve):
        rows = (wbuf if solve else qbuf)[p * wide:(p + 1) * wide, :]
        into, den_into = (ebuf, dbuf) if solve else (fbuf, fden)
        limit = (lax.broadcasted_iota(jnp.int32, (8, wide), 1) + p * wide
                 - lax.broadcasted_iota(jnp.int32, (8, wide), 0))
        top = jnp.full((8, wide), 0.0 if solve else MASKED, F32)
        tiles = 2 * p + 2
        for j in range(tiles):
            score = lax.dot_general(kbuf[j * BLK:(j + 1) * BLK, :], rows, NT, preferred_element_type=F32)
            score = (score + bias[tile_of(p, j)]).reshape(BLK // 8, 8, wide)
            if j >= 2 * p:
                key = lax.broadcasted_iota(jnp.int32, score.shape, 0) * 8 + j * BLK
                score = jnp.where((key < limit) if solve else (key <= limit), score, MASKED)
            top = jnp.maximum(top, jnp.max(score, axis=0))
            sscr[j * BLK:(j + 1) * BLK, :] = score.reshape(BLK, wide)
        peak = jnp.max(top, axis=0, keepdims=True)
        total = jnp.zeros((8, wide), F32)
        for j in range(tiles):
            e = jnp.exp2((sscr[j * BLK:(j + 1) * BLK, :] - peak) * SCALE2)
            total = total + jnp.sum(e.reshape(BLK // 8, 8, wide), axis=0)
            into[p, j * BLK:(j + 1) * BLK, :] = e.astype(BF16)
            if solve and j >= 2 * p:
                mbuf[p, (j - 2 * p) * BLK:(j - 2 * p + 1) * BLK, :] = e
        den = jnp.sum(total, axis=0, keepdims=True)
        if solve:
            den = den + jnp.exp2(-peak * SCALE2)
        den_into[p] = 1.0 / den
        if solve:
            mbuf[p] = mbuf[p] * den_into[p]

    def diagonal(x):
        zero = jnp.zeros((BLK, BLK), BF16)
        return jnp.concatenate([jnp.concatenate([x[:, :BLK], zero], axis=1),
                                jnp.concatenate([zero, x[:, BLK:]], axis=1)], axis=0)

    def split(x):
        hi = x.astype(BF16)
        return hi, (x - hi.astype(F32)).astype(BF16)

    def product(a, b):
        (a_hi, a_lo), (b_hi, b_lo) = split(a), split(b)
        return dot(jnp.concatenate([a_hi, a_lo, a_hi], axis=1), jnp.concatenate([b_hi, b_hi, b_lo], axis=0))

    def invert(p):
        eye = (lax.broadcasted_iota(jnp.int32, (BLK, BLK), 0)
               == lax.broadcasted_iota(jnp.int32, (BLK, BLK), 1)).astype(F32)
        eye = jnp.concatenate([eye, eye], axis=1)
        upper = jnp.concatenate([mbuf[p, :BLK, :BLK], mbuf[p, BLK:, BLK:]], axis=1)
        parts = split(upper)
        total = eye - upper
        power = dot(parts[0], diagonal(parts[0])).astype(BF16)
        yield
        for step in range(1, 7):
            if step < 6:
                both = dot(jnp.concatenate([total.astype(BF16), power], axis=0), diagonal(power))
                total = total + both[:BLK]
                power = both[BLK:].astype(BF16)
            else:
                total = total + dot(total.astype(BF16), diagonal(power))
            yield
        guess = total.astype(BF16)
        again = dot(jnp.concatenate(parts, axis=0), diagonal(guess))
        yield
        residual = eye - guess.astype(F32) - again[:BLK] - again[BLK:]
        better = guess.astype(F32) + dot(guess, diagonal(residual.astype(BF16)))
        yield
        inner = product(mbuf[p, :BLK, BLK:], better[:, BLK:])
        yield
        corner = -product(better[:, :BLK], inner)
        whole = jnp.concatenate(
            [jnp.concatenate([better[:, :BLK], corner], axis=1),
             jnp.concatenate([jnp.zeros((BLK, BLK), F32), better[:, BLK:]], axis=1)], axis=0)
        hi, lo = split(whole)
        ybuf[p, :wide] = hi
        ybuf[p, wide:2 * wide] = hi
        ybuf[p, 2 * wide:] = lo

    def solved(first, last):
        return jnp.concatenate([ubuf[q] for q in range(first, last)], axis=1)

    def passed(buf, p, first, last):
        return dot(solved(first, last), buf[p, first * wide:last * wide, :])

    def chain(p, known, known_to):
        rhs = vbuf[p * wide:(p + 1) * wide, :].astype(F32).T
        if p > known_to:
            fresh = passed(ebuf, p, known_to, p)
            known = fresh if known is None else known + fresh
        if known is not None:
            rhs = rhs - known * dbuf[p]
        hi, lo = split(rhs)
        ubuf[p] = dot(jnp.concatenate([hi, lo, hi], axis=1), ybuf[p]).astype(BF16)

    def together(steps):
        steps = list(steps)
        while steps:
            steps = [one for one in steps if next(one, True) is None]

    def readout_copy(p, r, half):
        return pltpu.make_async_remote_copy(
            src_ref=obuf.at[p, pl.ds((2 * r + half) * HALF, HALF)], dst_ref=strip(out_ref, me),
            send_sem=o_send.at[2 * p + r, half], recv_sem=o_recv, device_id={"seq": 2 * p + r, "head": half},
            device_id_type=MESH)

    def read(p, known, known_to):
        out = passed(fbuf, p, known_to, p + 1)
        if known is not None:
            out = out + known
        obuf[p] = (out * fden[p]).T.astype(BF16)
        for r in (0, 1):
            for half in (0, 1):
                own = (me == 2 * p + r) & (core == half)

                @pl.when(jnp.logical_not(own))
                def _():
                    readout_copy(p, r, half).start()

                @pl.when(own)
                def _():
                    pltpu.make_async_copy(obuf.at[p, pl.ds((2 * r + half) * HALF, HALF)], strip(out_ref, me),
                                          o_recv).start()

    @pl.when(core == 1)
    def _():
        wait_all(sbuf, st_recv)
        mask(range(pairs - 1))
        wait_rows(kbuf, 0, 0, n // 2)
        keys_over().start()
        wait_rows(wbuf, 1, 0, n // 2)
        for p in range(half_pairs):
            weights(p, True)
        together([invert(p) for p in range(half_pairs)])
        wait_rows(vbuf, 2, 0, n // 2)
        for p in range(half_pairs):
            chain(p, None, 0)
            solved_over(p).start()
        wait_all(kbuf.at[n * HALF:], k_recv)
        wait_rows(qbuf, 3, n // 2, n - 2)
        for p in range(half_pairs, pairs - 1):
            weights(p, False)
        wait_rows(qbuf, 3, 0, n // 2)
        for p in range(half_pairs):
            weights(p, False)
            read(p, None, 0)
        for p in range(half_pairs, pairs - 1):
            known = passed(fbuf, p, 0, p)
            wait_all(ubuf.at[p], u_recv.at[p])
            read(p, known, p)

    @pl.when(core == 0)
    def _():
        last = pairs - 1
        wait_all(sbuf, st_recv)
        mask(range(half_pairs, pairs))
        wait_rows(kbuf, 0, n // 2, n)
        keys_over().start()
        wait_all(kbuf.at[:n * HALF], k_recv)
        wait_rows(wbuf, 1, n // 2, n)
        for p in range(half_pairs, pairs):
            weights(p, True)
        together([invert(p) for p in range(half_pairs, pairs)])
        wait_rows(qbuf, 3, n - 2, n)
        weights(last, False)
        for p in range(half_pairs):
            wait_all(ubuf.at[p], u_recv.at[p])
        known = {p: passed(ebuf, p, 0, half_pairs) for p in range(half_pairs, pairs)}
        known_read = passed(fbuf, last, 0, half_pairs)
        wait_rows(vbuf, 2, n // 2, n)
        for p in range(half_pairs, pairs):
            chain(p, known[p], half_pairs)
            if p < last:
                solved_over(p).start()
        read(last, known_read, half_pairs)

    for stream in range(4):
        @pl.when(core != streams[stream][2])
        def _():
            remote(stream, 0).wait_send()

        def sent(step, carry):
            remote(stream, step).wait_send()
            return carry

        lax.fori_loop(1, n, sent, 0)
    for c in (0, 1):
        @pl.when(core == c)
        def _():
            def starts_sent(step, carry):
                starts_copy(step, c).wait_send()
                return carry

            lax.fori_loop(1, n, starts_sent, 0)

    keys_over().wait_send()

    def sent_by(solves, reads):
        for p in solves:
            solved_over(p).wait_send()
        for p in reads:
            for r in (0, 1):
                for half in (0, 1):
                    @pl.when(jnp.logical_not((me == 2 * p + r) & (core == half)))
                    def _():
                        readout_copy(p, r, half).wait_send()

    @pl.when(core == 1)
    def _():
        sent_by(range(half_pairs), range(pairs - 1))

    @pl.when(core == 0)
    def _():
        sent_by(range(half_pairs, pairs - 1), (pairs - 1,))

    wait_all(out_ref, o_recv)


def solution(mesh):
    n = mesh.shape["seq"]

    def step(queries, keys, writes, values, starts):
        features = queries.shape[1]
        length = n * BLK
        hbm = pl.BlockSpec(memory_space=pl.ANY)
        dma = pltpu.SemaphoreType.DMA
        return pl.pallas_call(
            functools.partial(kernel, n),
            out_shape=jax.ShapeDtypeStruct((HALF, features), BF16),
            in_specs=[hbm] * 5,
            out_specs=hbm,
            scratch_shapes=[
                pltpu.VMEM((length, HD), BF16),
                pltpu.VMEM((length, HD), BF16),
                pltpu.VMEM((length, HD), BF16),
                pltpu.VMEM((length, HD), BF16),
                pltpu.VMEM((n, 1, BLK), jnp.int32),
                pltpu.VMEM((n // 2 * (n // 2 + 1), BLK, 2 * BLK), F32),
                pltpu.VMEM((n // 2, length, 2 * BLK), BF16),
                pltpu.VMEM((n // 2, length, 2 * BLK), BF16),
                pltpu.VMEM((length, 2 * BLK), F32),
                pltpu.VMEM((n // 2, 2 * BLK, 2 * BLK), F32),
                pltpu.VMEM((n // 2, 6 * BLK, 2 * BLK), BF16),
                pltpu.VMEM((n // 2, HD, 2 * BLK), BF16),
                pltpu.VMEM((n // 2, 2 * BLK, HD), BF16),
                pltpu.VMEM((n // 2, 1, 2 * BLK), F32),
                pltpu.VMEM((n // 2, 1, 2 * BLK), F32),
                dma((4, n)),
                dma((n, 2)),
                dma((4, 2)),
                dma,
                dma,
                dma,
                dma((n // 2,)),
                dma((n // 2,)),
                dma((n, 2)),
                dma,
            ],
            compiler_params=pltpu.CompilerParams(collective_id=0, has_side_effects=True,
                                                 vmem_limit_bytes=67_043_328),
        )(queries, keys, writes, values, starts.reshape(1, BLK))

    rows = P(("dp", "seq", "head"), None)
    return jax.shard_map(step, mesh=mesh, in_specs=(rows, rows, rows, rows, P(("dp", "seq"))), out_specs=rows,
                         check_vma=False)
```

time: 34.7 us -> 32.6 us (0.939)
  Pallas kernels: 32.9 us -> 30.8 us
    pallas_call x1, Pallas kernels: 32.9 us -> 30.8 us  [step(): pl.pallas_call(functools.partial(kernel, n), out_shape=jax.ShapeDtypeStru...]
where the time goes in v3:
time: 32.6 us; the launch traced here: 32.5 us
  Pallas kernels  30.8 us (94%)
  local copies, waits for them, and re-layouts  1.67 us (5%)
    pallas_call x1, Pallas kernels, step(): pl.pallas_call(functools.partial(kernel, n), out_shape=jax.ShapeDtypeStru...  30.8 us
    unnamed x1, local copies, waits for them, and re-layouts  1.67 us

profile of v3, /device:TPU:1, one launch (start us, length us, event | category | flops | bytes accessed | tf_op | source)
XLA Modules:
  0.0 32.5 jit_solution(10055242837790023211)
XLA Ops:
  0.0 30.8 %shard_map.55 = bf16[64,2048]{1,0:T(8,128)(2,1)} custom-call(bf16[64,2048]{1,0:T(8,128)(2,1)} %q_ref.1, bf16[64,2048]{1,0:T(8,128)(2,1)} %k_ref.1, bf16[64,2048]{1,0:T(8,128)(2,1)} %w_ref.1, bf16[64,2048]{1,0:T(8,128)(2,1)} %v_ref.1, s32[1,128]{1,0:T(1,128)} %bitcast.1), custom_call_target="tpu_custom_call" | custom-call | tf_op jit(solution)/shard_map/pallas_call | solution.py:364
  30.8 1.7 %copy.7 = bf16[64,2048]{1,0:T(8,128)(2,1)} copy(bf16[64,2048]{1,0:T(8,128)(2,1)} %shard_map.55) | data formatting | bytes 524288

commit v4 on v3

--- a/solution.py
+++ b/solution.py
@@ -46,7 +46,12 @@
     my_rows = pl.ds(pl.multiple_of(me * BLK + core * HALF, HALF), HALF)
     half_index = me // (n // 2)
     solver = 1 - half_index
-    reader = jnp.where(me >= n - 2, 0, 1)
+    pairs = n // 2
+    late = (6, 7) if pairs == 8 else (pairs - 1,)
+    early = tuple(p for p in range(pairs) if p not in late)
+    reader = 1
+    for p in late:
+        reader = jnp.where(me // 2 == p, 0, reader)
     streams = ((k_ref, kbuf, solver), (w_ref, wbuf, solver), (v_ref, vbuf, solver), (q_ref, qbuf, reader))
 
     def strip(ref, head):
@@ -57,7 +62,7 @@
         target = chip(step)
         return pltpu.make_async_remote_copy(
             src_ref=strip(src, target), dst_ref=dst.at[my_rows], send_sem=send_sem.at[stream, step],
-            recv_sem=recv_sem.at[stream, half_index], device_id={"seq": target, "head": c}, device_id_type=MESH)
+            recv_sem=recv_sem.at[stream], device_id={"seq": target, "head": c}, device_id_type=MESH)
 
     def starts_copy(step, c):
         return pltpu.make_async_remote_copy(
@@ -79,7 +84,7 @@
 
         @pl.when(core == c)
         def _():
-            pltpu.make_async_copy(strip(src, me), dst.at[my_rows], recv_sem.at[stream, half_index]).start()
+            pltpu.make_async_copy(strip(src, me), dst.at[my_rows], recv_sem.at[stream]).start()
 
         @pl.when(core != c)
         def _():
@@ -91,25 +96,14 @@
 
         lax.fori_loop(1, n, send, 0)
 
-    send_stream(0)
-    send_stream(1)
-
-    @pl.when(half_index == 0)
-    def _():
-        send_stream(2)
-        send_stream(3)
-
-    @pl.when(half_index != 0)
-    def _():
-        send_stream(3)
-        send_stream(2)
+    for stream in range(4):
+        send_stream(stream)
 
     def wait_all(buf, sem):
         pltpu.make_async_copy(buf, buf, sem).wait()
 
-    def wait_rows(buf, stream, first, last):
-        if last > first:
-            wait_all(buf.at[first * BLK:last * BLK], recv_sem.at[stream, first // (n // 2)])
+    def wait_blocks(buf, stream, count):
+        wait_all(buf.at[:count * BLK], recv_sem.at[stream])
 
     def keys_over():
         mine = kbuf.at[pl.ds(pl.multiple_of((1 - core) * (n * HALF), n * HALF), n * HALF)]
@@ -121,7 +115,6 @@
             src_ref=ubuf.at[p], dst_ref=ubuf.at[p], send_sem=u_send.at[p], recv_sem=u_recv.at[p],
             device_id={"head": 1 - core}, device_id_type=MESH)
 
-    pairs = n // 2
     wide = 2 * BLK
 
     half_pairs = pairs // 2
@@ -176,18 +169,14 @@
         hi = x.astype(BF16)
         return hi, (x - hi.astype(F32)).astype(BF16)
 
-    def product(a, b):
-        (a_hi, a_lo), (b_hi, b_lo) = split(a), split(b)
-        return dot(jnp.concatenate([a_hi, a_lo, a_hi], axis=1), jnp.concatenate([b_hi, b_hi, b_lo], axis=0))
-
     def invert(p):
         eye = (lax.broadcasted_iota(jnp.int32, (BLK, BLK), 0)
                == lax.broadcasted_iota(jnp.int32, (BLK, BLK), 1)).astype(F32)
         eye = jnp.concatenate([eye, eye], axis=1)
         upper = jnp.concatenate([mbuf[p, :BLK, :BLK], mbuf[p, BLK:, BLK:]], axis=1)
-        parts = split(upper)
+        low, rest = split(upper)
         total = eye - upper
-        power = dot(parts[0], diagonal(parts[0])).astype(BF16)
+        power = dot(low, diagonal(low)).astype(BF16)
         yield
         for step in range(1, 7):
             if step < 6:
@@ -198,21 +187,20 @@
                 total = total + dot(total.astype(BF16), diagonal(power))
             yield
         guess = total.astype(BF16)
-        again = dot(jnp.concatenate(parts, axis=0), diagonal(guess))
+        again = dot(jnp.concatenate([low, rest], axis=0), diagonal(guess))
         yield
         residual = eye - guess.astype(F32) - again[:BLK] - again[BLK:]
-        better = guess.astype(F32) + dot(guess, diagonal(residual.astype(BF16)))
+        better, finer = split(guess.astype(F32) + dot(guess, diagonal(residual.astype(BF16))))
         yield
-        inner = product(mbuf[p, :BLK, BLK:], better[:, BLK:])
+        inner = dot(mbuf[p, :BLK, BLK:].astype(BF16), better[:, BLK:]).astype(BF16)
         yield
-        corner = -product(better[:, :BLK], inner)
-        whole = jnp.concatenate(
-            [jnp.concatenate([better[:, :BLK], corner], axis=1),
-             jnp.concatenate([jnp.zeros((BLK, BLK), F32), better[:, BLK:]], axis=1)], axis=0)
-        hi, lo = split(whole)
-        ybuf[p, :wide] = hi
-        ybuf[p, wide:2 * wide] = hi
-        ybuf[p, 2 * wide:] = lo
+        corner, finer_corner = split(-dot(better[:, :BLK], inner))
+        zero = jnp.zeros((BLK, BLK), BF16)
+        for k, (x, c) in enumerate(((better, corner), (finer, finer_corner))):
+            ybuf[p, k, :BLK, :BLK] = x[:, :BLK]
+            ybuf[p, k, :BLK, BLK:] = c
+            ybuf[p, k, BLK:, :BLK] = zero
+            ybuf[p, k, BLK:, BLK:] = x[:, BLK:]
 
     def solved(first, last):
         return jnp.concatenate([ubuf[q] for q in range(first, last)], axis=1)
@@ -220,15 +208,17 @@
     def passed(buf, p, first, last):
         return dot(solved(first, last), buf[p, first * wide:last * wide, :])
 
-    def chain(p, known, known_to):
+    def chain(p, sums):
         rhs = vbuf[p * wide:(p + 1) * wide, :].astype(F32).T
-        if p > known_to:
-            fresh = passed(ebuf, p, known_to, p)
-            known = fresh if known is None else known + fresh
-        if known is not None:
-            rhs = rhs - known * dbuf[p]
+        if p in sums:
+            rhs = rhs - sums[p] * dbuf[p]
         hi, lo = split(rhs)
-        ubuf[p] = dot(jnp.concatenate([hi, lo, hi], axis=1), ybuf[p]).astype(BF16)
+        ubuf[p] = (dot(hi, ybuf[p, 0]) + dot(hi, ybuf[p, 1]) + lo.astype(F32)).astype(BF16)
+
+    def pass_on(q, which, sums):
+        for p in which:
+            more = passed(ebuf, p, q, q + 1)
+            sums[p] = sums[p] + more if p in sums else more
 
     def together(steps):
         steps = list(steps)
@@ -241,11 +231,8 @@
             send_sem=o_send.at[2 * p + r, half], recv_sem=o_recv, device_id={"seq": 2 * p + r, "head": half},
             device_id_type=MESH)
 
-    def read(p, known, known_to):
-        out = passed(fbuf, p, known_to, p + 1)
-        if known is not None:
-            out = out + known
-        obuf[p] = (out * fden[p]).T.astype(BF16)
+    def read(p):
+        obuf[p] = (passed(fbuf, p, 0, p + 1) * fden[p]).T.astype(BF16)
         for r in (0, 1):
             for half in (0, 1):
                 own = (me == 2 * p + r) & (core == half)
@@ -262,54 +249,52 @@
     @pl.when(core == 1)
     def _():
         wait_all(sbuf, st_recv)
-        mask(range(pairs - 1))
-        wait_rows(kbuf, 0, 0, n // 2)
+        mask(sorted(set(range(half_pairs)) | set(early)))
+        wait_blocks(kbuf, 0, n // 2)
         keys_over().start()
-        wait_rows(wbuf, 1, 0, n // 2)
+        wait_blocks(wbuf, 1, n // 2)
         for p in range(half_pairs):
             weights(p, True)
         together([invert(p) for p in range(half_pairs)])
-        wait_rows(vbuf, 2, 0, n // 2)
+        wait_blocks(vbuf, 2, n // 2)
+        sums = {}
         for p in range(half_pairs):
-            chain(p, None, 0)
+            chain(p, sums)
             solved_over(p).start()
+            pass_on(p, range(p + 1, half_pairs), sums)
         wait_all(kbuf.at[n * HALF:], k_recv)
-        wait_rows(qbuf, 3, n // 2, n - 2)
-        for p in range(half_pairs, pairs - 1):
+        wait_blocks(qbuf, 3, 2 * len(early))
+        for p in early:
             weights(p, False)
-        wait_rows(qbuf, 3, 0, n // 2)
-        for p in range(half_pairs):
-            weights(p, False)
-            read(p, None, 0)
-        for p in range(half_pairs, pairs - 1):
-            known = passed(fbuf, p, 0, p)
-            wait_all(ubuf.at[p], u_recv.at[p])
-            read(p, known, p)
+            if p >= half_pairs:
+                wait_all(ubuf.at[p], u_recv.at[p])
+            read(p)
 
     @pl.when(core == 0)
     def _():
-        last = pairs - 1
         wait_all(sbuf, st_recv)
-        mask(range(half_pairs, pairs))
-        wait_rows(kbuf, 0, n // 2, n)
+        mask(sorted(set(range(half_pairs, pairs)) | set(late)))
+        wait_blocks(kbuf, 0, n // 2)
         keys_over().start()
         wait_all(kbuf.at[:n * HALF], k_recv)
-        wait_rows(wbuf, 1, n // 2, n)
+        wait_blocks(wbuf, 1, n // 2)
         for p in range(half_pairs, pairs):
             weights(p, True)
         together([invert(p) for p in range(half_pairs, pairs)])
-        wait_rows(qbuf, 3, n - 2, n)
-        weights(last, False)
-        for p in range(half_pairs):
-            wait_all(ubuf.at[p], u_recv.at[p])
-        known = {p: passed(ebuf, p, 0, half_pairs) for p in range(half_pairs, pairs)}
-        known_read = passed(fbuf, last, 0, half_pairs)
-        wait_rows(vbuf, 2, n // 2, n)
+        wait_blocks(vbuf, 2, n // 2)
+        sums = {}
+        for q in range(half_pairs):
+            wait_all(ubuf.at[q], u_recv.at[q])
+            pass_on(q, range(half_pairs, pairs), sums)
         for p in range(half_pairs, pairs):
-            chain(p, known[p], half_pairs)
-            if p < last:
+            chain(p, sums)
+            if p in early:
                 solved_over(p).start()
-        read(last, known_read, half_pairs)
+            pass_on(p, range(p + 1, pairs), sums)
+        wait_blocks(qbuf, 3, 2 * len(late))
+        for p in late:
+            weights(p, False)
+            read(p)
 
     for stream in range(4):
         @pl.when(core != streams[stream][2])
@@ -344,11 +329,11 @@
 
     @pl.when(core == 1)
     def _():
-        sent_by(range(half_pairs), range(pairs - 1))
+        sent_by(range(half_pairs), early)
 
     @pl.when(core == 0)
     def _():
-        sent_by(range(half_pairs, pairs - 1), (pairs - 1,))
+        sent_by([p for p in early if p >= half_pairs], late)
 
     wait_all(out_ref, o_recv)
 
@@ -377,14 +362,14 @@
                 pltpu.VMEM((n // 2, length, 2 * BLK), BF16),
                 pltpu.VMEM((length, 2 * BLK), F32),
                 pltpu.VMEM((n // 2, 2 * BLK, 2 * BLK), F32),
-                pltpu.VMEM((n // 2, 6 * BLK, 2 * BLK), BF16),
+                pltpu.VMEM((n // 2, 2, 2 * BLK, 2 * BLK), BF16),
                 pltpu.VMEM((n // 2, HD, 2 * BLK), BF16),
                 pltpu.VMEM((n // 2, 2 * BLK, HD), BF16),
                 pltpu.VMEM((n // 2, 1, 2 * BLK), F32),
                 pltpu.VMEM((n // 2, 1, 2 * BLK), F32),
                 dma((4, n)),
                 dma((n, 2)),
-                dma((4, 2)),
+                dma((4,)),
                 dma,
                 dma,
                 dma,
@@ -394,8 +379,9 @@
                 dma,
             ],
             compiler_params=pltpu.CompilerParams(collective_id=0, has_side_effects=True,
-                                                 vmem_limit_bytes=67_043_328),
-        )(queries, keys, writes, values, starts.reshape(1, BLK))
+                                                 vmem_limit_bytes=48 * 1024 * 1024),
+        )(*(pltpu.with_memory_space_constraint(x, pltpu.HBM)
+            for x in (queries, keys, writes, values, starts.reshape(1, BLK))))
 
     rows = P(("dp", "seq", "head"), None)
     return jax.shard_map(step, mesh=mesh, in_specs=(rows, rows, rows, rows, P(("dp", "seq"))), out_specs=rows,

time: 32.6 us -> 29.7 us (0.911)
  Pallas kernels: 30.8 us -> 28.6 us
  local copies, waits for them, and re-layouts: 1.67 us -> 0.71 us
    pallas_call x1, Pallas kernels: 30.8 us -> 28.6 us  [step(): pl.pallas_call(functools.partial(kernel, n), out_shape=jax.ShapeDtypeStru...]
    unnamed x1, local copies, waits for them, and re-layouts: 1.67 us -> 0.71 us
where the time goes in v4:
time: 29.7 us; the launch traced here: 29.3 us
  Pallas kernels  28.6 us (96%)
  local copies, waits for them, and re-layouts  0.71 us (2%)
    pallas_call x1, Pallas kernels, step(): pl.pallas_call(functools.partial(kernel, n), out_shape=jax.ShapeDtypeStru...  28.6 us
    unnamed x1, local copies, waits for them, and re-layouts  0.71 us

profile of v4, /device:TPU:1, one launch (start us, length us, event | category | flops | bytes accessed | tf_op | source)
XLA Modules:
  0.0 29.3 jit_solution(13092171201021818843)
XLA Ops:
  0.0 28.6 %shard_map.55 = bf16[64,2048]{1,0:T(8,128)(2,1)S(1)} custom-call(bf16[64,2048]{1,0:T(8,128)(2,1)} %q_ref.1, bf16[64,2048]{1,0:T(8,128)(2,1)} %k_ref.1, bf16[64,2048]{1,0:T(8,128)(2,1)} %w_ref.1, bf16[64,2048]{1,0:T(8,128)(2,1)} %v_ref.1, s32[1,128]{1,0:T(1,128)} %bitcast.1), custom_call_target="tpu_custom_call" | custom-call | tf_op jit(solution)/shard_map/pallas_call | solution.py:349
  28.6 0.7 %copy.7 = bf16[64,2048]{1,0:T(8,128)(2,1)} copy(bf16[64,2048]{1,0:T(8,128)(2,1)S(1)} %shard_map.55) | data formatting | bytes 524288

commit v5 on v4

--- a/solution.py
+++ b/solution.py
@@ -34,12 +34,10 @@
 
     barrier = pltpu.get_barrier_semaphore()
 
-    def greet(step, carry):
+    far = [10, 9, 11, 6, 14, 5, 7, 13, 15, 2, 8, 1, 3, 4, 12]
+    for step in [step for step in far if step < n] + list(range(16, n)):
         for c in (0, 1):
             pl.semaphore_signal(barrier, inc=1, device_id={"seq": chip(step), "head": c}, device_id_type=MESH)
-        return carry
-
-    lax.fori_loop(1, n, greet, 0)
     pl.semaphore_signal(barrier, inc=1, device_id={"head": 1 - core}, device_id_type=MESH)
     pl.semaphore_wait(barrier, 2 * n - 1)
 
@@ -69,10 +67,20 @@
             src_ref=st_ref, dst_ref=sbuf.at[me], send_sem=st_send.at[step, c], recv_sem=st_recv,
             device_id={"seq": chip(step), "head": c}, device_id_type=MESH)
 
-    pltpu.make_async_copy(st_ref, sbuf.at[me], st_recv).start()
+    rows_on = ([p for p in range(pairs) if p >= pairs // 2 or p in late],
+               [p for p in range(pairs) if p < pairs // 2 or p in early])
+    wanted = []
     for c in (0, 1):
-        @pl.when(core == c)
+        found = me < 0
+        for p in rows_on[c]:
+            found = found | (me // 2 == p)
+        wanted.append(found)
+
+    for c in (0, 1):
+        @pl.when((core == c) & wanted[c])
         def _():
+            pltpu.make_async_copy(st_ref, sbuf.at[me], st_recv).start()
+
             def send_starts(step, carry):
                 starts_copy(step, c).start()
                 return carry
@@ -233,6 +241,8 @@
 
     def read(p):
         obuf[p] = (passed(fbuf, p, 0, p + 1) * fden[p]).T.astype(BF16)
+
+    def hand_out(p):
         for r in (0, 1):
             for half in (0, 1):
                 own = (me == 2 * p + r) & (core == half)
@@ -246,9 +256,19 @@
                     pltpu.make_async_copy(obuf.at[p, pl.ds((2 * r + half) * HALF, HALF)], strip(out_ref, me),
                                           o_recv).start()
 
+    def read_out(which, awaited):
+        for p in which:
+            weights(p, False)
+        for p in awaited:
+            wait_all(ubuf.at[p], u_recv.at[p])
+        for p in which:
+            read(p)
+        for p in which:
+            hand_out(p)
+
     @pl.when(core == 1)
     def _():
-        wait_all(sbuf, st_recv)
+        wait_all(sbuf.at[:2 * len(rows_on[1])], st_recv)
         mask(sorted(set(range(half_pairs)) | set(early)))
         wait_blocks(kbuf, 0, n // 2)
         keys_over().start()
@@ -264,15 +284,12 @@
             pass_on(p, range(p + 1, half_pairs), sums)
         wait_all(kbuf.at[n * HALF:], k_recv)
         wait_blocks(qbuf, 3, 2 * len(early))
-        for p in early:
-            weights(p, False)
-            if p >= half_pairs:
-                wait_all(ubuf.at[p], u_recv.at[p])
-            read(p)
+        for k in range(0, len(early), 2):
+            read_out(early[k:k + 2], [p for p in early[k:k + 2] if p >= half_pairs])
 
     @pl.when(core == 0)
     def _():
-        wait_all(sbuf, st_recv)
+        wait_all(sbuf.at[:2 * len(rows_on[0])], st_recv)
         mask(sorted(set(range(half_pairs, pairs)) | set(late)))
         wait_blocks(kbuf, 0, n // 2)
         keys_over().start()
@@ -293,8 +310,7 @@
             pass_on(p, range(p + 1, pairs), sums)
         wait_blocks(qbuf, 3, 2 * len(late))
         for p in late:
-            weights(p, False)
-            read(p)
+            read_out((p,), ())
 
     for stream in range(4):
         @pl.when(core != streams[stream][2])
@@ -307,7 +323,7 @@
 
         lax.fori_loop(1, n, sent, 0)
     for c in (0, 1):
-        @pl.when(core == c)
+        @pl.when((core == c) & wanted[c])
         def _():
             def starts_sent(step, carry):
                 starts_copy(step, c).wait_send()

time: 29.7 us -> 29.6 us (level)
  no operation moved by 1% of the time
where the time goes in v5:
time: 29.6 us; the launch traced here: 29.5 us
  Pallas kernels  28.7 us (97%)
  local copies, waits for them, and re-layouts  0.71 us (2%)
    pallas_call x1, Pallas kernels, step(): pl.pallas_call(functools.partial(kernel, n), out_shape=jax.ShapeDtypeStru...  28.7 us
    unnamed x1, local copies, waits for them, and re-layouts  0.71 us

profile of v5, /device:TPU:1, one launch (start us, length us, event | category | flops | bytes accessed | tf_op | source)
XLA Modules:
  0.0 29.5 jit_solution(11798801092496769956)
XLA Ops:
  0.0 28.7 %shard_map.55 = bf16[64,2048]{1,0:T(8,128)(2,1)S(1)} custom-call(bf16[64,2048]{1,0:T(8,128)(2,1)} %q_ref.1, bf16[64,2048]{1,0:T(8,128)(2,1)} %k_ref.1, bf16[64,2048]{1,0:T(8,128)(2,1)} %w_ref.1, bf16[64,2048]{1,0:T(8,128)(2,1)} %v_ref.1, s32[1,128]{1,0:T(1,128)} %bitcast.1), custom_call_target="tpu_custom_call" | custom-call | tf_op jit(solution)/shard_map/pallas_call | solution.py:365
  28.8 0.7 %copy.7 = bf16[64,2048]{1,0:T(8,128)(2,1)} copy(bf16[64,2048]{1,0:T(8,128)(2,1)S(1)} %shard_map.55) | data formatting | bytes 524288

commit v6 on v5

--- a/solution.py
+++ b/solution.py
@@ -217,7 +217,7 @@
         return dot(solved(first, last), buf[p, first * wide:last * wide, :])
 
     def chain(p, sums):
-        rhs = vbuf[p * wide:(p + 1) * wide, :].astype(F32).T
+        rhs = vbuf[p * wide:(p + 1) * wide, :].T.astype(F32)
         if p in sums:
             rhs = rhs - sums[p] * dbuf[p]
         hi, lo = split(rhs)
@@ -240,7 +240,7 @@
             device_id_type=MESH)
 
     def read(p):
-        obuf[p] = (passed(fbuf, p, 0, p + 1) * fden[p]).T.astype(BF16)
+        obuf[p] = (passed(fbuf, p, 0, p + 1) * fden[p]).astype(BF16).T
 
     def hand_out(p):
         for r in (0, 1):

time: 29.6 us -> 29.6 us (level)
  no operation moved by 1% of the time
where the time goes in v6:
time: 29.6 us; the launch traced here: 29.5 us
  Pallas kernels  28.7 us (97%)
  local copies, waits for them, and re-layouts  0.71 us (2%)
    pallas_call x1, Pallas kernels, step(): pl.pallas_call(functools.partial(kernel, n), out_shape=jax.ShapeDtypeStru...  28.7 us
    unnamed x1, local copies, waits for them, and re-layouts  0.71 us

profile of v6, /device:TPU:1, one launch (start us, length us, event | category | flops | bytes accessed | tf_op | source)
XLA Modules:
  0.0 29.5 jit_solution(7472662425157355933)
XLA Ops:
  0.0 28.7 %shard_map.55 = bf16[64,2048]{1,0:T(8,128)(2,1)S(1)} custom-call(bf16[64,2048]{1,0:T(8,128)(2,1)} %q_ref.1, bf16[64,2048]{1,0:T(8,128)(2,1)} %k_ref.1, bf16[64,2048]{1,0:T(8,128)(2,1)} %w_ref.1, bf16[64,2048]{1,0:T(8,128)(2,1)} %v_ref.1, s32[1,128]{1,0:T(1,128)} %bitcast.1), custom_call_target="tpu_custom_call" | custom-call | tf_op jit(solution)/shard_map/pallas_call | solution.py:365
  28.7 0.7 %copy.7 = bf16[64,2048]{1,0:T(8,128)(2,1)} copy(bf16[64,2048]{1,0:T(8,128)(2,1)S(1)} %shard_map.55) | data formatting | bytes 524288
